TPU v7x, 32 devices: a whole 2x2x4 slice. The times are simulated.
32 devices in a mesh: dp: 8 (over y, x, core), chan: 4 (over z).
Axes of the slice: x: 2, y: 2, z: 4, core: 2. Of those that a mesh axis runs over, the one named last changes fastest.
Arguments:
- inputs: bfloat16 [192, 152, 800], P('dp', None, 'chan'), may hold values from -6 to 6
- ocean_mask: int32 [192, 152], P('dp'), may hold values 0 or 1
- counts: int32 [4], replicated, may hold values from 1 to 2
- kernel: float32 [7, 7, 800], P(None, None, 'chan'), may hold values from -0.875 to 0.875
- conv_bias: float32 [800], P('chan'), may hold values from -3 to 3
- norm_gain: float32 [800], P('chan'), may hold values from 0.5 to 1.5
- norm_bias: float32 [800], P('chan'), may hold values from -3 to 3
- weight_in: bfloat16 [800, 3200], P(None, 'chan'), may hold values from -0.21875 to 0.21875
- bias_in: float32 [3200], P('chan'), may hold values from -3 to 3
- weight_out: bfloat16 [3200, 800], P('chan'), may hold values from -0.21875 to 0.21875
- bias_out: float32 [800], P('chan'), may hold values from -3 to 3
- cotangent: bfloat16 [192, 152, 800], P('dp', None, 'chan'), may hold values from -6 to 6
Outputs:
- output: bfloat16 [192, 152, 800], P('dp', None, 'chan')
- grad_inputs: float32 [192, 152, 800], P('dp', None, 'chan')
- grad_kernel: float32 [7, 7, 800], P(None, None, 'chan')
- grad_conv_bias: float32 [800], P('chan')
- grad_gain: float32 [800], P('chan')
- grad_norm_bias: float32 [800], P('chan')
- grad_weight_in: float32 [800, 3200], P(None, 'chan')
- grad_bias_in: float32 [3200], P('chan')
- grad_weight_out: float32 [3200, 800], P('chan')
- grad_bias_out: float32 [800], P('chan')
All inputs are finite; a program needn't handle non-finite values. No bound on the sum of `ocean_mask` on one device may be relied on, other than what follows from the above.
Results may differ from a plain program's by a relative error of at most 0.0057.
Values may be sent and summed in bfloat16 or wider, within the bound.
No kernel may reach another device: no remote copies, remote signals or barrier semaphores. Data moves between devices by JAX's collectives and lax.ppermute only.
A program may use at most 192 MiB of HBM per device.

v0:
```python
import jax
import jax.numpy as jnp
from jax import lax
from jax.sharding import PartitionSpec as P

CH = 800
GROUPS = 8
HISTORY = 2
SPAN = 2


EPSILON = 1e-05


def swapped(block, axis, distance):
    count = lax.axis_size(axis)
    route = []
    for low in range(count):
        high = low | 1 << distance
        if high != low and high < count:
            route += [(low, high), (high, low)]
    return lax.ppermute(block, axis, route)


def with_rim(values, rim, top_valid, bottom_valid):
    return jnp.concatenate([rim * top_valid, values, rim * bottom_valid], axis=0)


def local_groups(values, group_size):
    height, across, local_ch = values.shape
    return jnp.sum(
        values.reshape(height, across, local_ch // group_size, group_size), axis=(0, 1, 3)
    )


def spread_groups(summed, group_size, members):
    return jnp.repeat(summed, group_size) / members


def gelu_slope(hidden):
    cumulative = 0.5 * (1.0 + lax.erf(hidden * 0.7071067811865476))
    density = jnp.exp(-0.5 * hidden * hidden) * 0.3989422804014327
    return cumulative + hidden * density


def body(
    inputs,
    ocean_mask,
    counts,
    kernel,
    conv_bias,
    norm_gain,
    norm_bias,
    weight_in,
    bias_in,
    weight_out,
    bias_out,
    cotangent,
):
    height, across, local_ch = inputs.shape
    pixels = height * across
    group_size = CH // GROUPS
    members = height * SPAN * across * group_size
    dp_index = lax.axis_index("dp")
    sample = dp_index // SPAN
    within = dp_index % SPAN
    sample_ids = jnp.arange(counts.shape[0])
    count_here = jnp.sum(jnp.where(sample_ids == sample, counts, 0))
    channel = lax.axis_index("chan") * local_ch + jnp.arange(local_ch)
    history_keep = (channel // (CH // HISTORY) < count_here).astype(jnp.float32)
    wet_cells = ocean_mask.astype(jnp.float32)[:, :, None]
    masked = inputs.astype(jnp.float32) * wet_cells * history_keep
    top_valid = (within > 0).astype(jnp.float32)
    bottom_valid = (within == 0).astype(jnp.float32)
    is_upper = within == 0
    masked_low = masked.astype(jnp.bfloat16)
    outgoing = jnp.where(is_upper, masked_low[height - 3 :], masked_low[:3])
    rim_in = swapped(outgoing, "dp", 0).astype(jnp.float32)
    padded = jnp.pad(with_rim(masked, rim_in, top_valid, bottom_valid), ((0, 0), (3, 3), (0, 0)))
    convolved = jnp.zeros((height, across, local_ch), jnp.float32) + conv_bias
    for row_shift in range(7):
        for col_shift in range(7):
            convolved = (
                convolved
                + padded[row_shift : row_shift + height, col_shift : col_shift + across]
                * kernel[row_shift, col_shift]
            )
    own_sum = local_groups(convolved, group_size)
    centre = spread_groups(own_sum + swapped(own_sum, "dp", 0), group_size, members)
    offset = convolved - centre
    own_sq = local_groups(offset * offset, group_size)
    spread = spread_groups(own_sq + swapped(own_sq, "dp", 0), group_size, members)
    inverse = lax.rsqrt(spread + EPSILON)
    standard = offset * inverse
    normed = (standard * norm_gain + norm_bias).astype(jnp.bfloat16).reshape(pixels, local_ch)
    grad_res = cotangent.astype(jnp.float32) * wet_cells
    grad_branch = grad_res.reshape(pixels, local_ch).astype(jnp.bfloat16)
    grad_bias_out = jnp.sum(grad_branch.astype(jnp.float32), 0)
    gathered = lax.all_gather(normed, "chan", axis=1, tiled=True)
    hidden = jnp.dot(gathered, weight_in, preferred_element_type=jnp.float32) + bias_in
    active = jax.nn.gelu(hidden, approximate=False).astype(jnp.bfloat16)
    partial_value = jnp.dot(active, weight_out, preferred_element_type=jnp.float32)
    branch = lax.psum_scatter(partial_value, "chan", scatter_dimension=1, tiled=True) + bias_out
    output = (wet_cells * (masked + branch.reshape(height, across, local_ch))).astype(jnp.bfloat16)
    grad_gathered = lax.all_gather(grad_branch, "chan", axis=1, tiled=True)
    grad_active = lax.dot_general(
        grad_gathered, weight_out, (((1,), (1,)), ((), ())), preferred_element_type=jnp.float32
    )
    grad_weight_out = lax.dot_general(
        active, grad_gathered, (((0,), (0,)), ((), ())), preferred_element_type=jnp.float32
    )
    grad_hidden = (grad_active * gelu_slope(hidden)).astype(jnp.bfloat16)
    grad_bias_in = jnp.sum(grad_hidden.astype(jnp.float32), 0)
    grad_weight_in = lax.dot_general(
        gathered, grad_hidden, (((0,), (0,)), ((), ())), preferred_element_type=jnp.float32
    )
    grad_part = lax.dot_general(
        grad_hidden, weight_in, (((1,), (1,)), ((), ())), preferred_element_type=jnp.float32
    )
    grad_normed = lax.psum_scatter(grad_part, "chan", scatter_dimension=1, tiled=True).reshape(
        height, across, local_ch
    )
    grad_gain = jnp.sum(grad_normed * standard, (0, 1))
    grad_norm_bias = jnp.sum(grad_normed, (0, 1))
    grad_standard = grad_normed * norm_gain
    own_pair = jnp.stack(
        [
            local_groups(grad_standard, group_size),
            local_groups(grad_standard * standard, group_size),
        ]
    )
    both_pair = own_pair + swapped(own_pair, "dp", 0)
    mean_first = spread_groups(both_pair[0], group_size, members)
    mean_second = spread_groups(both_pair[1], group_size, members)
    grad_conv = inverse * (grad_standard - mean_first - standard * mean_second)
    grad_conv_bias = jnp.sum(grad_conv, (0, 1))
    kernel_rows = []
    for row_shift in range(7):
        for col_shift in range(7):
            kernel_rows.append(
                jnp.sum(
                    grad_conv
                    * padded[row_shift : row_shift + height, col_shift : col_shift + across],
                    (0, 1),
                )
            )
    grad_kernel = jnp.stack(kernel_rows).reshape(7, 7, local_ch)
    grad_out_rows = jnp.where(is_upper, grad_conv[height - 3 :], grad_conv[:3])
    grad_rim = swapped(grad_out_rows.astype(jnp.bfloat16), "dp", 0).astype(grad_out_rows.dtype)
    grad_padded = jnp.pad(
        with_rim(grad_conv, grad_rim, top_valid, bottom_valid), ((0, 0), (3, 3), (0, 0))
    )
    grad_masked = jnp.zeros((height, across, local_ch), jnp.float32)
    for row_shift in range(7):
        for col_shift in range(7):
            grad_masked = (
                grad_masked
                + grad_padded[
                    6 - row_shift : 6 - row_shift + height, 6 - col_shift : 6 - col_shift + across
                ]
                * kernel[row_shift, col_shift]
            )
    grad_inputs = wet_cells * history_keep * (grad_res + grad_masked)
    (
        grad_kernel,
        grad_conv_bias,
        grad_gain,
        grad_norm_bias,
        grad_weight_in,
        grad_bias_in,
        grad_weight_out,
        grad_bias_out,
    ) = lax.psum(
        (
            grad_kernel,
            grad_conv_bias,
            grad_gain,
            grad_norm_bias,
            grad_weight_in,
            grad_bias_in,
            grad_weight_out,
            grad_bias_out,
        ),
        "dp",
    )
    return (
        output,
        grad_inputs,
        grad_kernel,
        grad_conv_bias,
        grad_gain,
        grad_norm_bias,
        grad_weight_in,
        grad_bias_in,
        grad_weight_out,
        grad_bias_out,
    )


def solution(mesh):
    in_specs = (
        P("dp", None, "chan"),
        P("dp", None),
        P(),
        P(None, None, "chan"),
        P("chan"),
        P("chan"),
        P("chan"),
        P(None, "chan"),
        P("chan"),
        P("chan", None),
        P("chan"),
        P("dp", None, "chan"),
    )
    out_specs = (
        P("dp", None, "chan"),
        P("dp", None, "chan"),
        P(None, None, "chan"),
        P("chan"),
        P("chan"),
        P("chan"),
        P(None, "chan"),
        P("chan"),
        P("chan", None),
        P("chan"),
    )
    return jax.shard_map(body, mesh=mesh, in_specs=in_specs, out_specs=out_specs, check_vma=False)
```

profile of v0, /device:TPU:0, one launch (start us, length us, event | category | flops | bytes accessed | tf_op | source)
XLA Modules:
  0.0 971.6 jit_solution(3660102376321455770)
XLA Ops:
  10.1 5.1 convert_reduce_fusion.1
  17.4 4.5 select_maximum_fusion.2
  22.3 75.7 %fusion.88 = (f32[200]{0:T(256)S(1)}, f32[24,152,200]{2,1,0:T(8,128)}) fusion(f32[200]{0:T(256)} %bitcast.48, f32[30,158,200]{2,1,0:T(8,128)} %select_maximum_fusion.2, f32[200]{0:T(256)} %bitcast.47, f32[200]{0:T(256)S(1)} %bitcast.130, f32[200]{0:T(256)S(1)} %bitcast.132, f32[3,152,200]{2,1,0:T(8,128)S(1)} %get-tuple-element.86, ...), kind=kLoop, calls=%fused_computation.242 | loop fusion | flops 76607800 | bytes 129180000 | tf_op jit(solution)/shard_map/reduce_sum | solution.py:31
  108.9 3.8 copy.33
  113.2 107.8 %all-gather.3.cloned.1.call-done = bf16[3648,800]{0,1:T(8,128)(2,1)} async-done(((bf16[3648,200]{0,1:T(8,128)(2,1)}), bf16[3648,800]{0,1:T(8,128)(2,1)}) %all-gather.3.cloned.1.call-update) | async-done | bytes 5836816 | tf_op jit(solution)/shard_map/all_gather | solution.py:99
  221.0 35.8 %fusion.2 = (bf16[3648,800]{0,1:T(8,128)(2,1)}, f32[3648,800]{0,1:T(8,128)}) fusion(f32[800]{0:T(1024)S(1)} %copy-done.101, bf16[3648,800]{0,1:T(8,128)(2,1)} %all-gather.3.cloned.1.call-done, bf16[800,800]{1,0:T(8,128)(2,1)S(1)} %copy-done), kind=kOutput, calls=%fused_computation.4 | convolution fusion | flops 4862054400 | bytes 24630400 | tf_op jit(solution)/shard_map/dot_general | solution.py:100
  256.8 74.2 %all-gather.5.cloned.1.call-done = bf16[3648,800]{0,1:T(8,128)(2,1)} async-done(((bf16[3648,200]{0,1:T(8,128)(2,1)}), bf16[3648,800]{0,1:T(8,128)(2,1)}) %all-gather.5.cloned.1.call-update) | async-done | bytes 5836816 | tf_op jit(solution)/shard_map/all_gather | solution.py:105
  331.0 12.0 %convert_reduce_fusion = (f32[800]{0:T(1024)S(1)}, bf16[3648,800]{0,1:T(8,128)(2,1)S(1)}) fusion(f32[3648,800]{0,1:T(8,128)} %get-tuple-element.141, f32[800]{0:T(1024)S(1)} %copy-done.101, bf16[800,800]{1,0:T(8,128)(2,1)} %param.21, bf16[3648,800]{0,1:T(8,128)(2,1)} %all-gather.5.cloned.1.call-done), kind=kOutput, calls=%fused_computation.11 | convolution fusion | flops 4707378176 | bytes 24633600 | tf_op jit(solution)/shard_map/dot_general | solution.py:106
  345.6 9.2 fusion.95
  356.3 11.5 %fusion.92 = f32[3648,800]{0,1:T(8,128)} fusion(bf16[3648,800]{0,1:T(8,128)(2,1)} %get-tuple-element.140, bf16[800,800]{1,0:T(8,128)(2,1)S(1)} %copy-done.100), kind=kOutput, calls=%fused_computation.246 | convolution fusion | flops 4669440000 | bytes 18790400 | tf_op jit(solution)/shard_map/dot_general | solution.py:102
  367.8 11.4 %fusion.94 = f32[800,800]{1,0:T(8,128)} fusion(bf16[3648,800]{0,1:T(8,128)(2,1)} %get-tuple-element.140, bf16[3648,800]{0,1:T(8,128)(2,1)} %all-gather.5.cloned.1.call-done), kind=kOutput, calls=%fused_computation.248 | convolution fusion | flops 4669440000 | bytes 14233600 | tf_op jit(solution)/shard_map/dot_general | solution.py:109
  379.2 11.5 %fusion.93 = f32[800,800]{1,0:T(8,128)} fusion(bf16[3648,800]{0,1:T(8,128)(2,1)} %all-gather.3.cloned.1.call-done, bf16[3648,800]{0,1:T(8,128)(2,1)} %copy-done.102), kind=kOutput, calls=%fused_computation.247 | convolution fusion | flops 4669440000 | bytes 14233600 | tf_op jit(solution)/shard_map/dot_general | solution.py:114
  390.7 164.1 %reduce-scatter.9.cloned.1.call-done = f32[3648,200]{0,1:T(8,128)} async-done(((f32[3648,800]{0,1:T(8,128)}), f32[3648,200]{0,1:T(8,128)}) %reduce-scatter.9.cloned.1.call-update) | async-done | bytes 2918416
  557.3 4.9 copy.34
  562.2 5.3 multiply_reduce_fusion
  567.8 191.2 %reduce-scatter.7.cloned.1.call-done = f32[3648,200]{0,1:T(8,128)} async-done(((f32[3648,800]{0,1:T(8,128)}), f32[3648,200]{0,1:T(8,128)}) %reduce-scatter.7.cloned.1.call-update) | async-done | bytes 2918416
  759.0 4.9 copy.32
  763.9 4.1 broadcast_add_fusion
  768.4 37.9 %multiply_reduce_fusion.1 = (f32[200]{0:T(256)S(1)}, f32[200]{0:T(256)S(1)}, f32[200]{0:T(256)S(1)}, f32[200]{0:T(256)S(1)}, f32[200]{0:T(256)S(1)}, /*index=5*/...) fusion(f32[30,158,200]{2,1,0:T(8,128)} %select_maximum_fusion.2, ...), kind=kLoop, calls=%fused_computation.162 | loop fusion | flops 31369200 | bytes 61304800 | tf_op jit(solution)/shard_map/reduce_sum | solution.py:141
  806.4 30.1 %multiply_reduce_fusion.2 = (f32[200]{0:T(256)S(1)}, f32[200]{0:T(256)S(1)}, f32[200]{0:T(256)S(1)}, f32[200]{0:T(256)S(1)}, f32[200]{0:T(256)S(1)}, /*index=5*/...) fusion(f32[24,152,200]{2,1,0:T(8,128)} %get-tuple-element.77, ...), kind=kLoop, calls=%fused_computation.163 | loop fusion | flops 26262000 | bytes 55464000 | tf_op jit(solution)/shard_map/reduce_sum | solution.py:141
  836.6 8.8 multiply_reduce_fusion.4
  849.1 26.5 %all-reduce.4 = (f32[7,7,200]{2,1,0:T(8,128)}, f32[200]{0:T(256)}, f32[200]{0:T(256)}, f32[200]{0:T(256)}, f32[800]{0:T(1024)}, /*index=5*/f32[200]{0:T(256)}) all-reduce(f32[7,7,200]{2,1,0:T(8,128)S(1)} %reshape.110, f32[200]{0:T(256)S(1)} %get-tuple-element.63, ...), channel_id=1, replica_groups=mesh['dp'=8,'chan'=4] {'dp'}, use_global_device_ids=true, to_apply=%region_60.61 | all-reduce | flops 11400 | bytes 91200 | tf_op jit(solution)/shard_map/psum | solution.py:173
  876.0 4.5 select_maximum_fusion
  880.8 78.5 %fusion.31 = f32[24,152,200]{2,1,0:T(8,128)} fusion(f32[24,152,200]{2,1,0:T(8,128)} %get-tuple-element.77, f32[3,152,200]{2,1,0:T(8,128)S(1)} %get-tuple-element.84, f32[3,152,200]{2,1,0:T(8,128)S(1)} %get-tuple-element.83, f32[30,158,200]{2,1,0:T(8,128)} %select_maximum_fusion, bf16[24,152,200]{2,1,0:T(8,128)(2,1)S(1)} %copy-done.5, f32[200]{0:T(256)} %bitcast.48, ...), kind=kLoop, calls=%fused_computation.64 | loop fusion | flops 78796800 | bytes 130652992 | tf_op jit(solution)/shard_map/mul | solution.py:163
  (272 shorter events, 32.6 us)
Async XLA Ops:
  7.2 213.8 %copy-start = (bf16[800,800]{1,0:T(8,128)(2,1)S(1)}, bf16[800,800]{1,0:T(8,128)(2,1)}, u32[]{:S(2)}) copy-start(bf16[800,800]{1,0:T(8,128)(2,1)} %param.19) | copy-start | bytes 3840004
  7.2 213.8 %all-gather.3.cloned.1.call-start = ((), (), s32[]{:S(2)}) async-start(), calls=%async_computation.2 | async-start | bytes 7424000 | tf_op jit(solution)/shard_map/all_gather | solution.py:99
  8.1 7.1 copy-start.11
  15.2 2.1 collective-permute-start
  98.2 1.2 collective-permute-start.1
  102.3 1.2 collective-permute-start.2
  108.8 112.2 %copy-start.101 = (f32[800]{0:T(1024)S(1)}, f32[800]{0:T(1024)}, u32[]{:S(2)}) copy-start(f32[800]{0:T(1024)} %param.20) | copy-start | bytes 9604
  108.8 222.2 %all-gather.5.cloned.1.call-start = ((), (), s32[]{:S(2)}) async-start(), calls=%async_computation.3 | async-start | bytes 7424000 | tf_op jit(solution)/shard_map/all_gather | solution.py:105
  112.7 442.1 %reduce-scatter.9.cloned.1.call-start = ((), (), s32[]{:S(2)}) async-start(), calls=%async_computation.5 | async-start | bytes 14848000
  354.9 404.1 %reduce-scatter.7.cloned.1.call-start = ((), (), s32[]{:S(2)}) async-start(), calls=%async_computation.4 | async-start | bytes 14848000
  367.8 591.6 %all-reduce.8.cloned.1.call-start = ((), (), s32[]{:S(2)}) async-start(), calls=%async_computation.6 | async-start | bytes 11468800 | tf_op jit(solution)/shard_map/psum | solution.py:173
  390.7 164.1 %copy-start.17 = (f32[200]{0:T(256)S(1)}, f32[200]{0:T(256)}, u32[]{:S(2)}) copy-start(f32[200]{0:T(256)} %param.17) | copy-start | bytes 2404
  567.5 196.4 %copy-start.98 = (f32[200]{0:T(256)S(1)}, f32[200]{0:T(256)}, u32[]{:S(2)}) copy-start(f32[200]{0:T(256)} %param.22) | copy-start | bytes 2404
  567.7 200.3 %collective-permute-start.3 = (f32[2,2]{1,0:T(2,128)S(1)}, f32[2,2]{1,0:T(2,128)S(1)}, u32[]{:S(2)}, u32[]{:S(2)}) collective-permute-start(f32[2,2]{1,0:T(2,128)S(1)} %pad_maximum_fusion.4), channel_id=1, source_target_pairs={{0,4},{4,0},{8,12},{12,8},{16,20},{20,16},{24,28},{28,24},{1,5},{5... | collective-permute-start | bytes 56 | tf_op jit(solution)/shard_map/ppermute | solution.py:22
  768.4 77.0 %slice-start = ((s8[4915200]{0:T(1024)(128)(4,1)}), s8[720896]{0:T(1024)(128)(4,1)S(1)}, s32[]{:S(2)}) async-start(s8[4915200]{0:T(1024)(128)(4,1)} %bitcast.121), calls=%async_computation.7 | async-start | bytes 1441792
  806.3 30.1 %copy-start.2 = (f32[24,152,200]{2,1,0:T(8,128)S(1)}, f32[24,152,200]{2,1,0:T(8,128)}, u32[]{:S(2)}) copy-start(f32[24,152,200]{2,1,0:T(8,128)} %get-tuple-element.77) | copy-start | bytes 8755204
  806.3 30.2 %copy-start.3 = (f32[24,152,200]{2,1,0:T(8,128)S(1)}, f32[24,152,200]{2,1,0:T(8,128)}, u32[]{:S(2)}) copy-start(f32[24,152,200]{2,1,0:T(8,128)} %get-tuple-element.137) | copy-start | bytes 8755204
  806.3 30.2 %copy-start.4 = (bf16[24,152,200]{2,1,0:T(8,128)(2,1)S(1)}, bf16[24,152,200]{2,1,0:T(8,128)(2,1)}, u32[]{:S(2)}) copy-start(bf16[24,152,200]{2,1,0:T(8,128)(2,1)} %param.12) | copy-start | bytes 4377604
  806.3 30.2 %copy-start.7 = (f32[3,152,200]{2,1,0:T(8,128)S(1)}, f32[3,152,200]{2,1,0:T(8,128)}, u32[]{:S(2)}) copy-start(f32[3,152,200]{2,1,0:T(8,128)} %copy-done.6) | copy-start | bytes 1094404
  806.4 30.2 %copy-start.9 = (f32[3,152,200]{2,1,0:T(8,128)S(1)}, f32[3,152,200]{2,1,0:T(8,128)}, u32[]{:S(2)}) copy-start(f32[3,152,200]{2,1,0:T(8,128)} %copy-done.8) | copy-start | bytes 1094404
  806.4 30.2 %copy-start.12 = (f32[24,152]{1,0:T(8,128)S(1)}, f32[24,152]{1,0:T(8,128)}, u32[]{:S(2)}) copy-start(f32[24,152]{1,0:T(8,128)} %copy-done.11) | copy-start | bytes 43780
  806.4 30.2 %copy-start.21 = (f32[200]{0:T(256)S(1)}, f32[200]{0:T(256)}, u32[]{:S(2)}) copy-start(f32[200]{0:T(256)} %copy-done.20) | copy-start | bytes 2404
  806.4 39.0 %slice-start.1 = ((s8[4915200]{0:T(1024)(128)(4,1)}), s8[4194304]{0:T(1024)(128)(4,1)S(1)}, s32[]{:S(2)}) async-start(s8[4915200]{0:T(1024)(128)(4,1)} %bitcast.121), calls=%async_computation.8 | async-start | bytes 8388608
  845.4 30.1 %collective-permute-start.4 = (bf16[3,152,200]{2,1,0:T(8,128)(2,1)S(1)}, bf16[3,152,200]{2,1,0:T(8,128)(2,1)S(1)}, u32[]{:S(2)}, u32[]{:S(2)}) collective-permute-start(bf16[3,152,200]{2,1,0:T(8,128)(2,1)S(1)} %fusion.83), channel_id=1, source_target_pairs={{0,4},{4,0},{8,12},{12,8},{16,20},{20,16},{24,28},{28,24},{1,5},{5... | collective-permute-start | bytes 547208 | tf_op jit(solution)/shard_map/ppermute | solution.py:22
  (91 other events, 477.4 us)
Sparse Core Ops, SparseCore 0:
  109.0 111.9 all-gather.2
  223.1 107.8 all-gather.4
  355.0 199.7 reduce-scatter.8
  557.0 201.9 reduce-scatter.6
  763.4 99.3 all-reduce.7
where the time goes:
time: 979 us; the launch traced here: 972 us
  waiting for transfers between devices  539 us (55%)
  other arithmetic  269 us (27%)
  matrix products  91.5 us (9%)
  local copies, waits for them, and re-layouts  27.8 us (3%)
  blocking collectives  26.5 us (3%)
  between operations  15.8 us (2%)
    unnamed x7, waiting for transfers between devices  355 us
    all_gather x1, waiting for transfers between devices, body(): gathered = lax.all_gather(normed, 'chan', axis=1, tiled=True)  108 us
    reduce_sum x4, other arithmetic, body(): jnp.sum(grad_conv * padded[row_shift:row_shift + height, col_shift:col_sh...  80.2 us
    reduce_sum x6, other arithmetic, local_groups(): jnp.sum(values.reshape(height, across, local_ch // group_size, group_size...  78.8 us
    mul x1, other arithmetic, body(): grad_inputs = wet_cells * history_keep * (grad_res + grad_masked)  78.5 us
    all_gather x1, waiting for transfers between devices, body(): grad_gathered = lax.all_gather(grad_branch, 'chan', axis=1, tiled=True)  74.2 us
    dot_general x1, matrix products, body(): jnp.dot(gathered, weight_in, preferred_element_type=jnp.float32) + bias_in  35.8 us
    psum x1, blocking collectives, body(): lax.psum((grad_kernel, grad_conv_bias, grad_gain, grad_norm_bias, grad_we...  26.5 us
  transfers between devices with their start and end apart: 10, of which 6 were waited for; matrix products, arithmetic and copies ran while one was open for 27% of the time, Pallas kernels for 0%

commit v1 on v0

v1 whole, which is shorter than its diff:
```python
import jax
import jax.numpy as jnp
from jax import lax
from jax.experimental import pallas as pl
from jax.experimental.pallas import tpu as pltpu
from jax.sharding import PartitionSpec as P

CH = 800
GROUPS = 8
HISTORY = 2
SPAN = 2
EPSILON = 1e-05
GROUP_SIZE = CH // GROUPS
PARTS = 4
ROW_BLOCK = 8
TILE = 256
F32 = jnp.float32
BF16 = jnp.bfloat16
VMEM = pl.BlockSpec(memory_space=pltpu.VMEM)
SMEM = pl.BlockSpec(memory_space=pltpu.SMEM)


def flipped(block, axis, bit):
    count = lax.axis_size(axis)
    return lax.ppermute(block, axis, [(place, place ^ bit) for place in range(count)])


def routed(block, allowed, partner):
    count, depth = lax.axis_size("dp"), lax.axis_size("chan")
    route = []
    for place in range(count):
        for level in range(depth):
            if allowed(place, level):
                to_place, to_level = partner(place, level)
                route.append((place * depth + level, to_place * depth + to_level))
    return lax.ppermute(block, ("dp", "chan"), route)


def lane_spans(channels):
    return [(start, min(128, channels - start)) for start in range(0, channels, 128)]


def by_lane_tile(rows):
    count, channels = rows.shape
    tiles = len(lane_spans(channels))
    padded = jnp.pad(rows, ((0, 0), (0, tiles * 128 - channels)))
    return padded.reshape(count, tiles, 128).transpose(1, 0, 2)


def frame(pad_ref, rim_ref, within, height, across, spans):
    top = jnp.where(within == 1, 0, height + 3)
    bottom = height + 3 - top
    for index in range(3):
        row = rim_ref[index].astype(F32)
        for tile, (start, width) in enumerate(spans):
            pad_ref[tile, top + index, 8 : 8 + across, 0:width] = row[:, start : start + width]
            pad_ref[tile, bottom + index] = jnp.zeros(pad_ref.shape[2:], F32)

    def sides(row, carry):
        for tile in range(len(spans)):
            pad_ref[tile, row, 0:8, :] = jnp.zeros((8, 128), F32)
            pad_ref[tile, row, 8 + across : 16 + across, :] = jnp.zeros((8, 128), F32)
        return carry

    lax.fori_loop(0, height + 6, sides, 0)


def depthwise_kernel(within_ref, x_ref, rim_ref, wet_ref, keep_ref, taps_ref, bias_ref, out_ref, stat_ref, pad_ref, sum_ref):
    height, across, channels = x_ref.shape
    spans = lane_spans(channels)
    frame(pad_ref, rim_ref, within_ref[0], height, across, spans)
    keep = keep_ref[...]

    def fill(row, carry):
        masked = x_ref[row].astype(F32) * wet_ref[row] * keep
        for tile, (start, width) in enumerate(spans):
            pad_ref[tile, row + 3, 8 : 8 + across, 0:width] = masked[:, start : start + width]
        return carry

    lax.fori_loop(0, height, fill, 0)
    sum_ref[...] = jnp.zeros_like(sum_ref)
    strips = across // 8
    for tile, (start, width) in enumerate(spans):

        def block(index, carry, tile=tile, start=start, width=width):
            row = index // strips * ROW_BLOCK
            col = pl.multiple_of(index % strips * 8, 8)
            acc = [jnp.broadcast_to(bias_ref[tile : tile + 1, :], (8, 128))] * ROW_BLOCK
            for b in range(7):
                rows = [pad_ref[tile, row + i, pl.ds(col + 5 + b, 8), :] for i in range(ROW_BLOCK + 6)]
                for a in range(7):
                    tap = jnp.broadcast_to(taps_ref[tile, a * 7 + b : a * 7 + b + 1, :], (8, 128))
                    for i in range(ROW_BLOCK):
                        acc[i] = acc[i] + rows[i + a] * tap
            total = acc[0]
            for i in range(ROW_BLOCK):
                out_ref[row + i, pl.ds(col, 8), start : start + width] = acc[i][:, :width]
                if i:
                    total = total + acc[i]
            sum_ref[tile] += total
            return carry

        lax.fori_loop(0, height // ROW_BLOCK * strips, block, 0)
    for tile, (start, width) in enumerate(spans):
        mean = jnp.sum(sum_ref[tile], axis=0, keepdims=True)[:, :width] / (height * across)

        def deviations(row, total, start=start, width=width, mean=mean):
            offset = out_ref[row, :, start : start + width] - mean
            return total + jnp.sum(offset * offset, axis=0, keepdims=True)

        stat_ref[0:1, start : start + width] = mean
        stat_ref[1:2, start : start + width] = lax.fori_loop(0, height, deviations, jnp.zeros((1, width), F32))


def depthwise(within, x, rim, wet, keep, taps, bias):
    height, across, channels = x.shape
    tiles = len(lane_spans(channels))
    return pl.pallas_call(
        depthwise_kernel,
        out_shape=(jax.ShapeDtypeStruct(x.shape, F32), jax.ShapeDtypeStruct((2, channels), F32)),
        in_specs=[SMEM] + [VMEM] * 6,
        out_specs=(VMEM, VMEM),
        scratch_shapes=[
            pltpu.VMEM((tiles, height + 6, across + 16, 128), F32),
            pltpu.VMEM((tiles, 8, 128), F32),
        ],
        compiler_params=pltpu.CompilerParams(vmem_limit_bytes=40 << 20),
        cost_estimate=pl.CostEstimate(flops=98 * x.size, bytes_accessed=6 * x.size, transcendentals=0),
        name="depthwise",
    )(within, x, rim, wet, keep, taps, bias)


def depthwise_back_kernel(
    within_ref, grad_ref, rim_ref, x_ref, cot_ref, wet_ref, keep_ref, taps_ref, out_ref, tap_grad_ref, pad_ref, acc_ref
):
    height, across, channels = x_ref.shape
    spans = lane_spans(channels)
    frame(pad_ref, rim_ref, within_ref[0], height, across, spans)

    def fill(row, carry):
        for tile, (start, width) in enumerate(spans):
            pad_ref[tile, row + 3, 8 : 8 + across, 0:width] = grad_ref[row, :, start : start + width]
        return carry

    lax.fori_loop(0, height, fill, 0)
    acc_ref[...] = jnp.zeros_like(acc_ref)
    strips = across // 8
    for tile, (start, width) in enumerate(spans):

        def block(index, carry, tile=tile, start=start, width=width):
            row = index // strips * ROW_BLOCK
            col = pl.multiple_of(index % strips * 8, 8)
            here = (pl.ds(col, 8), slice(start, start + width))
            keep = jnp.broadcast_to(keep_ref[0:1, start : start + width], (8, width))
            mask = [wet_ref[row + i, pl.ds(col, 8), :] * keep for i in range(ROW_BLOCK)]
            masked = [x_ref[row + i, here[0], here[1]].astype(F32) * mask[i] for i in range(ROW_BLOCK)]
            acc = [cot_ref[row + i, here[0], here[1]].astype(F32) for i in range(ROW_BLOCK)]
            for b in range(7):
                rows = [pad_ref[tile, row + i, pl.ds(col + 5 + b, 8), 0:width] for i in range(ROW_BLOCK + 6)]
                for a in range(7):
                    index_of_tap = (6 - a) * 7 + (6 - b)
                    tap = jnp.broadcast_to(taps_ref[tile, index_of_tap : index_of_tap + 1, 0:width], (8, width))
                    total = None
                    for i in range(ROW_BLOCK):
                        acc[i] = acc[i] + rows[i + a] * tap
                        product = rows[i + a] * masked[i]
                        total = product if total is None else total + product
                    acc_ref[tile, index_of_tap, :, 0:width] += total
            for i in range(ROW_BLOCK):
                out_ref[row + i, here[0], here[1]] = acc[i] * mask[i]
            return carry

        lax.fori_loop(0, height // ROW_BLOCK * strips, block, 0)
    for tile, (start, width) in enumerate(spans):
        tap_grad_ref[:, start : start + width] = jnp.sum(acc_ref[tile], axis=1)[:, 0:width]


def depthwise_back(within, grad, rim, x, cot, wet, keep, taps):
    height, across, channels = x.shape
    tiles = len(lane_spans(channels))
    return pl.pallas_call(
        depthwise_back_kernel,
        out_shape=(jax.ShapeDtypeStruct(x.shape, F32), jax.ShapeDtypeStruct((49, channels), F32)),
        in_specs=[SMEM] + [VMEM] * 7,
        out_specs=(VMEM, VMEM),
        scratch_shapes=[
            pltpu.VMEM((tiles, height + 6, across + 16, 128), F32),
            pltpu.VMEM((tiles, 49, 8, 128), F32),
        ],
        compiler_params=pltpu.CompilerParams(vmem_limit_bytes=50 << 20),
        cost_estimate=pl.CostEstimate(flops=196 * x.size, bytes_accessed=12 * x.size, transcendentals=0),
        name="depthwise_back",
    )(within, grad, rim, x, cot, wet, keep, taps)


def group_total(row):
    channels = row.shape[1]
    group = lax.broadcasted_iota(jnp.int32, (1, channels), 1) // GROUP_SIZE
    total = jnp.zeros((1, channels), F32)
    for index in range(channels // GROUP_SIZE):
        member = group == index
        total = jnp.where(member, jnp.sum(jnp.where(member, row, 0.0), axis=1, keepdims=True), total)
    return total


def cut_kernel(level_ref, cot_ref, wet_ref, *refs):
    blocks, bias_ref = refs[:PARTS], refs[PARTS]
    height, across, channels = cot_ref.shape
    rows = height // PARTS
    total = jnp.zeros((8, channels), F32)
    for k in range(PARTS):
        first = (level_ref[0] ^ k) * rows

        def one(row, total, k=k, first=first):
            grad = (cot_ref[first + row].astype(F32) * wet_ref[first + row]).astype(BF16)
            blocks[k][pl.ds(row * across, across), :] = grad
            return total + jnp.sum(grad.astype(F32).reshape(across // 8, 8, channels), axis=0)

        total = lax.fori_loop(0, rows, one, total)
    bias_ref[...] = jnp.sum(total, axis=0, keepdims=True)


def cut(level, cot, wet):
    height, across, channels = cot.shape
    block = jax.ShapeDtypeStruct((height // PARTS * across, channels), BF16)
    return pl.pallas_call(
        cut_kernel,
        out_shape=(block,) * PARTS + (jax.ShapeDtypeStruct((1, channels), F32),),
        in_specs=[SMEM, VMEM, VMEM],
        out_specs=(VMEM,) * (PARTS + 1),
        compiler_params=pltpu.CompilerParams(vmem_limit_bytes=30 << 20),
        cost_estimate=pl.CostEstimate(flops=2 * cot.size, bytes_accessed=4 * cot.size, transcendentals=0),
        name="cut",
    )(level, cot, wet)


def norm_kernel(level_ref, conv_ref, stat_ref, other_ref, gain_ref, bias_ref, *refs):
    blocks, fit_ref = refs[:PARTS], refs[PARTS]
    height, across, channels = conv_ref.shape
    rows = height // PARTS
    cells = height * across
    stat, other = stat_ref[...], other_ref[...]
    members = SPAN * GROUP_SIZE
    centre = group_total(stat[0:1] + other[0:1]) / members
    away, other_away = stat[0:1] - centre, other[0:1] - centre
    squares = stat[1:2] + other[1:2] + cells * (away * away + other_away * other_away)
    inverse = lax.rsqrt(group_total(squares) / (members * cells) + EPSILON)
    fit_ref[0:1] = centre
    fit_ref[1:2] = inverse
    gain, bias = gain_ref[...], bias_ref[...]
    for k in range(PARTS):
        first = (level_ref[0] ^ k) * rows

        def one(row, carry, k=k, first=first):
            standard = (conv_ref[first + row] - centre) * inverse
            blocks[k][pl.ds(row * across, across), :] = (standard * gain + bias).astype(BF16)
            return carry

        lax.fori_loop(0, rows, one, 0)


def norm(level, conv, stat, other, gain, bias):
    height, across, channels = conv.shape
    block = jax.ShapeDtypeStruct((height // PARTS * across, channels), BF16)
    return pl.pallas_call(
        norm_kernel,
        out_shape=(block,) * PARTS + (jax.ShapeDtypeStruct((2, channels), F32),),
        in_specs=[SMEM] + [VMEM] * 5,
        out_specs=(VMEM,) * (PARTS + 1),
        compiler_params=pltpu.CompilerParams(vmem_limit_bytes=30 << 20),
        cost_estimate=pl.CostEstimate(flops=4 * conv.size, bytes_accessed=6 * conv.size, transcendentals=0),
        name="norm",
    )(level, conv, stat, other, gain, bias)


def moments_kernel(level_ref, conv_ref, fit_ref, *refs):
    blocks, sums_ref = refs[:PARTS], refs[PARTS]
    height, across, channels = conv_ref.shape
    rows = height // PARTS
    centre, inverse = fit_ref[0:1], fit_ref[1:2]
    first_sum = jnp.zeros((8, channels), F32)
    second_sum = jnp.zeros((8, channels), F32)
    for k in range(PARTS):
        first = (level_ref[0] ^ k) * rows

        def one(row, sums, k=k, first=first):
            standard = (conv_ref[first + row] - centre) * inverse
            grad = blocks[k][pl.ds(row * across, across), :].astype(F32)
            fold = lambda v: jnp.sum(v.reshape(across // 8, 8, channels), axis=0)
            return sums[0] + fold(grad), sums[1] + fold(grad * standard)

        first_sum, second_sum = lax.fori_loop(0, rows, one, (first_sum, second_sum))
    sums_ref[0:1] = jnp.sum(first_sum, axis=0, keepdims=True)
    sums_ref[1:2] = jnp.sum(second_sum, axis=0, keepdims=True)


def moments(level, conv, fit, blocks):
    channels = conv.shape[2]
    return pl.pallas_call(
        moments_kernel,
        out_shape=jax.ShapeDtypeStruct((2, channels), F32),
        in_specs=[SMEM] + [VMEM] * (2 + PARTS),
        out_specs=VMEM,
        compiler_params=pltpu.CompilerParams(vmem_limit_bytes=30 << 20),
        cost_estimate=pl.CostEstimate(flops=6 * conv.size, bytes_accessed=6 * conv.size, transcendentals=0),
        name="moments",
    )(level, conv, fit, *blocks)


def norm_back_kernel(level_ref, within_ref, conv_ref, fit_ref, sums_ref, other_ref, gain_ref, *refs):
    blocks, (grad_ref, rim_ref, bias_ref) = refs[:PARTS], refs[PARTS:]
    height, across, channels = conv_ref.shape
    rows = height // PARTS
    members = SPAN * GROUP_SIZE * height * across
    centre, inverse = fit_ref[0:1], fit_ref[1:2]
    gain = gain_ref[...]
    sums = sums_ref[...] + other_ref[...]
    mean_first = group_total(sums[0:1] * gain) / members
    mean_second = group_total(sums[1:2] * gain) / members
    total = jnp.zeros((8, channels), F32)
    for k in range(PARTS):
        first = (level_ref[0] ^ k) * rows

        def one(row, total, k=k, first=first):
            standard = (conv_ref[first + row] - centre) * inverse
            grad = blocks[k][pl.ds(row * across, across), :].astype(F32)
            grad = inverse * (grad * gain - mean_first - standard * mean_second)
            grad_ref[first + row] = grad
            return total + jnp.sum(grad.reshape(across // 8, 8, channels), axis=0)

        total = lax.fori_loop(0, rows, one, total)
    bias_ref[...] = jnp.sum(total, axis=0, keepdims=True)
    edge = jnp.where(within_ref[0] == 0, height - 3, 0)
    for index in range(3):
        rim_ref[index] = grad_ref[edge + index].astype(BF16)


def norm_back(level, within, conv, fit, sums, other, gain, blocks):
    height, across, channels = conv.shape
    return pl.pallas_call(
        norm_back_kernel,
        out_shape=(
            jax.ShapeDtypeStruct(conv.shape, F32),
            jax.ShapeDtypeStruct((3, across, channels), BF16),
            jax.ShapeDtypeStruct((1, channels), F32),
        ),
        in_specs=[SMEM, SMEM] + [VMEM] * (5 + PARTS),
        out_specs=(VMEM,) * 3,
        compiler_params=pltpu.CompilerParams(vmem_limit_bytes=30 << 20),
        cost_estimate=pl.CostEstimate(flops=8 * conv.size, bytes_accessed=10 * conv.size, transcendentals=0),
        name="norm_back",
    )(level, within, conv, fit, sums, other, gain, *blocks)


def finish_kernel(level_ref, x_ref, wet_ref, keep_ref, bias_ref, *refs):
    blocks, out_ref = refs[:PARTS], refs[PARTS]
    height, across, channels = x_ref.shape
    rows = height // PARTS
    keep, bias = keep_ref[...], bias_ref[...]
    for k in range(PARTS):
        first = (level_ref[0] ^ k) * rows

        def one(row, carry, k=k, first=first):
            branch = blocks[k][pl.ds(row * across, across), :].astype(F32) + bias
            masked = x_ref[first + row].astype(F32) * keep
            out_ref[first + row] = (wet_ref[first + row] * (masked + branch)).astype(BF16)
            return carry

        lax.fori_loop(0, rows, one, 0)


def finish(level, x, wet, keep, bias, blocks):
    return pl.pallas_call(
        finish_kernel,
        out_shape=jax.ShapeDtypeStruct(x.shape, BF16),
        in_specs=[SMEM] + [VMEM] * (4 + PARTS),
        out_specs=VMEM,
        compiler_params=pltpu.CompilerParams(vmem_limit_bytes=30 << 20),
        cost_estimate=pl.CostEstimate(flops=4 * x.size, bytes_accessed=8 * x.size, transcendentals=0),
        name="finish",
    )(level, x, wet, keep, bias, *blocks)


def pointwise_kernel(twist_ref, *refs):
    acts = refs[: 4 * PARTS]
    win_ref, wout_ref, bias_ref = refs[4 * PARTS : 4 * PARTS + 3]
    outs = refs[4 * PARTS + 3 : 4 * PARTS + 11]
    grad_own_ref, grad_far_ref, own_ref, far_ref, in_keep_ref, in_send_ref, out_keep_ref, out_send_ref = outs
    turned_ref, turned_grad_ref, back_ref, branch_ref, hidden_ref, slope_ref, active_ref, grad_hidden_ref = refs[
        4 * PARTS + 11 :
    ]
    twist = twist_ref[0]
    cells, channels = acts[0].shape
    normed = (acts[:PARTS], acts[PARTS : 2 * PARTS])
    grads = (acts[2 * PARTS : 3 * PARTS], acts[3 * PARTS :])

    @pl.when(pl.program_id(0) == 0)
    def _():
        for side in range(2):
            for k in range(PARTS):
                turned_ref[side, k, 0:channels, :] = normed[side][k][...].T
                ones = (lax.broadcasted_iota(jnp.int32, (8, cells), 0) == 0).astype(BF16)
                turned_ref[side, k, channels : channels + 8, :] = ones
                turned_grad_ref[side, k] = grads[side][k][...].T
        back_ref[...] = jnp.zeros_like(back_ref)
        branch_ref[...] = jnp.zeros_like(branch_ref)

    for side in range(2):
        hidden = jnp.broadcast_to(bias_ref[...], (cells, TILE))
        grad = jnp.zeros((cells, TILE), F32)
        for k in range(PARTS):
            hidden = hidden + jnp.dot(normed[side][k][...], win_ref[twist ^ k], preferred_element_type=F32)
            grad = grad + jnp.dot(grads[side][k][...], wout_ref[twist ^ k], preferred_element_type=F32)
        hidden_ref[side] = hidden
        slope_ref[side] = grad
        value = hidden_ref[side]
        cumulative = 0.5 * (1.0 + lax.erf(value * 0.7071067811865476))
        density = jnp.exp(-0.5 * value * value) * 0.3989422804014327
        active_ref[side] = (value * cumulative).astype(BF16)
        grad_hidden_ref[side] = (slope_ref[side] * (cumulative + value * density)).astype(BF16)
        dims = (((1,), (1,)), ((), ()))
        for k in range(PARTS):
            branch_ref[side, k] += lax.dot_general(
                active_ref[side], wout_ref[twist ^ k], dims, preferred_element_type=F32
            )
            back_ref[side, k] += lax.dot_general(
                grad_hidden_ref[side], win_ref[twist ^ k], dims, preferred_element_type=F32
            )
    for j in range(PARTS):
        k = twist ^ j
        grad_in = jnp.dot(turned_ref[0, k], grad_hidden_ref[0], preferred_element_type=F32) + jnp.dot(
            turned_ref[1, k], grad_hidden_ref[1], preferred_element_type=F32
        )
        grad_out = jnp.dot(turned_grad_ref[0, k], active_ref[0], preferred_element_type=F32) + jnp.dot(
            turned_grad_ref[1, k], active_ref[1], preferred_element_type=F32
        )
        if j % 2 == 0:
            in_keep_ref[j // 2] = grad_in
        else:
            in_send_ref[j // 2] = grad_in.astype(BF16)
        if j < 2:
            out_keep_ref[j] = grad_out
        else:
            out_send_ref[j - 2] = grad_out.astype(BF16)

    @pl.when(pl.program_id(0) == pl.num_programs(0) - 1)
    def _():
        grad_own_ref[...] = back_ref[0].astype(BF16)
        grad_far_ref[...] = back_ref[1].astype(BF16)
        own_ref[...] = branch_ref[0].astype(BF16)
        far_ref[...] = branch_ref[1].astype(BF16)


def pointwise(twist, acts, win, wout, bias, units):
    cells, channels = acts[0].shape
    whole = lambda *shape: pl.BlockSpec(shape, lambda t: (0,) * len(shape), pipeline_mode=pl.Buffered(1))
    tiled = lambda *shape: pl.BlockSpec(shape + (TILE,), lambda t: (0,) * len(shape) + (t,))
    quad = jax.ShapeDtypeStruct((PARTS, cells, channels), BF16)
    return pl.pallas_call(
        pointwise_kernel,
        grid=(win.shape[2] // TILE,),
        out_shape=(quad,) * 4
        + (
            jax.ShapeDtypeStruct((2, channels + 8, units), F32),
            jax.ShapeDtypeStruct((2, channels + 8, units), BF16),
            jax.ShapeDtypeStruct((2, channels, units), F32),
            jax.ShapeDtypeStruct((2, channels, units), BF16),
        ),
        in_specs=[SMEM]
        + [whole(cells, channels)] * (4 * PARTS)
        + [tiled(PARTS, channels), tiled(PARTS, channels), tiled(1)],
        out_specs=(whole(PARTS, cells, channels),) * 4
        + (tiled(2, channels + 8), tiled(2, channels + 8), tiled(2, channels), tiled(2, channels)),
        scratch_shapes=[
            pltpu.VMEM((2, PARTS, channels + 8, cells), BF16),
            pltpu.VMEM((2, PARTS, channels, cells), BF16),
            pltpu.VMEM((2, PARTS, cells, channels), F32),
            pltpu.VMEM((2, PARTS, cells, channels), F32),
            pltpu.VMEM((2, cells, TILE), F32),
            pltpu.VMEM((2, cells, TILE), F32),
            pltpu.VMEM((2, cells, TILE), BF16),
            pltpu.VMEM((2, cells, TILE), BF16),
        ],
        compiler_params=pltpu.CompilerParams(vmem_limit_bytes=60 << 20, dimension_semantics=("arbitrary",)),
        cost_estimate=pl.CostEstimate(
            flops=24 * cells * PARTS * channels * units, bytes_accessed=40 << 20, transcendentals=4 * cells * units
        ),
        name="pointwise",
    )(twist, *acts, win, wout, bias)


def picked(stack, index):
    return lax.dynamic_index_in_dim(stack, index, 0, keepdims=False)


def body(
    inputs,
    ocean_mask,
    counts,
    kernel,
    conv_bias,
    norm_gain,
    norm_bias,
    weight_in,
    bias_in,
    weight_out,
    bias_out,
    cotangent,
):
    height, across, channels = inputs.shape
    units = weight_in.shape[1]
    place = lax.axis_index("dp")
    level = lax.axis_index("chan")
    core = place % SPAN
    quarter = place // SPAN % PARTS
    mine = level // 2 == core
    scalar = lambda value: value.astype(jnp.int32).reshape(1)
    core_of = lambda at: at % SPAN

    part = channels
    piece = jnp.stack(
        [
            lax.dynamic_slice_in_dim(weight_in, quarter * part, part, 0),
            lax.dynamic_slice_in_dim(weight_out, quarter * part, part, 1).T,
        ]
    )
    owner = lambda at, lev: lev // 2 == core_of(at)
    near = [
        tuple(
            routed(value, owner, lambda at, lev, k=k: (at, lev ^ k)) for value in (piece, bias_in.reshape(1, units))
        )
        for k in (1, 2, 3)
    ]
    first = [jnp.where(mine, own, far) for own, far in zip((piece, bias_in.reshape(1, units)), near[1])]
    second = [jnp.where(mine, one, far) for one, far in zip(near[0], near[2])]
    slab = jnp.concatenate([first[0], second[0]], axis=2)
    win_rows = [slab[0]]
    wout_rows = [slab[1]]
    win_rows += [flipped(win_rows[0], "dp", 2)]
    win_rows += [flipped(value, "dp", 4) for value in win_rows]
    across_wout = flipped(wout_rows[0], "dp", 4)
    wout_rows = [wout_rows[0], flipped(wout_rows[0], "dp", 2), across_wout, flipped(across_wout, "dp", 2)]
    room = -2 * units % TILE
    widen = lambda rows: jnp.pad(jnp.stack(rows), ((0, 0), (0, 0), (0, room)))
    win, wout = widen(win_rows), widen(wout_rows)
    bias_hidden = jnp.pad(jnp.concatenate([first[1], second[1]], axis=1), ((0, 0), (0, room)))

    sample = place // SPAN
    count_here = jnp.sum(jnp.where(jnp.arange(counts.shape[0]) == sample, counts, 0))
    channel = level * channels + jnp.arange(channels)
    keep = (channel // (CH // HISTORY) < count_here).astype(F32).reshape(1, channels)
    wet = ocean_mask.astype(F32)[:, :, None]
    edge = jnp.where(core == 0, height - 3, 0)
    outgoing = (
        lax.dynamic_slice_in_dim(inputs, edge, 3, 0).astype(F32) * lax.dynamic_slice_in_dim(wet, edge, 3, 0) * keep
    ).astype(BF16)
    rim = flipped(outgoing, "dp", 1)
    taps = by_lane_tile(kernel.reshape(49, channels))
    row = lambda vector: vector.reshape(1, channels)
    conv, stat = depthwise(scalar(core), inputs, rim, wet, keep, taps, by_lane_tile(row(conv_bias))[:, 0])
    *grad_blocks, grad_bias_out = cut(scalar(level), cotangent, wet)
    *normed_blocks, fit = norm(scalar(level), conv, stat, flipped(stat, "dp", 1), row(norm_gain), row(norm_bias))

    spread_out = lambda blocks: [blocks[0]] + [flipped(blocks[k], "chan", k) for k in range(1, PARTS)]
    grad_cells = spread_out(grad_blocks)
    normed_cells = spread_out(normed_blocks)
    other_core = lambda blocks: [flipped(block, "dp", 1) for block in blocks]
    acts = normed_cells + other_core(normed_cells) + grad_cells + other_core(grad_cells)
    back_own, back_far, branch_own, branch_far, in_keep, in_send, out_keep, out_send = pointwise(
        scalar(level ^ quarter), acts, win, wout, bias_hidden, 2 * units
    )
    joined = lambda own, far: [
        (own[k].astype(F32) + far[k].astype(F32)).astype(BF16) for k in range(PARTS)
    ]
    back_blocks = spread_out(joined(back_own, flipped(back_far, "dp", 1)))
    branch_blocks = spread_out(joined(branch_own, flipped(branch_far, "dp", 1)))

    sums = moments(scalar(level), conv, fit, back_blocks)
    grad_conv, outgoing_grad, grad_conv_bias = norm_back(
        scalar(level), scalar(core), conv, fit, sums, flipped(sums, "dp", 1), row(norm_gain), back_blocks
    )
    grad_rim = flipped(outgoing_grad, "dp", 1)
    grad_inputs, grad_taps = depthwise_back(scalar(core), grad_conv, grad_rim, inputs, cotangent, wet, keep, taps)
    output = finish(scalar(level), inputs, wet, keep, row(bias_out), branch_blocks)
    small = jnp.concatenate([grad_taps, grad_conv_bias, sums[1:2], sums[0:1], grad_bias_out, jnp.zeros((3, channels), F32)])
    bit = 1
    while bit < lax.axis_size("dp"):
        small = small + flipped(small, "dp", bit)
        bit *= 2

    wide = lambda value: value.astype(F32)
    in_two = in_keep + wide(flipped(in_send, "dp", 2))
    out_two = out_keep + wide(flipped(out_send, "dp", 4))
    in_one = in_two[0] + wide(flipped(in_two[1].astype(BF16), "dp", 4))
    out_one = out_two[0] + wide(flipped(out_two[1].astype(BF16), "dp", 2))
    both = jnp.concatenate([in_one, out_one])
    low = both.astype(BF16)
    stranger = lambda at, lev: not owner(at, lev)
    total = (
        both[:, :units]
        + wide(routed(low[:, units:], owner, lambda at, lev: (at, lev ^ 1)))
        + wide(routed(low[:, :units], stranger, lambda at, lev: (at, lev ^ 2)))
        + wide(routed(low[:, units:], stranger, lambda at, lev: (at, lev ^ 3)))
    )
    bit = SPAN * PARTS
    while bit < lax.axis_size("dp"):
        total = total + flipped(total, "dp", bit)
        bit *= 2
    held = total.astype(BF16)
    held = jnp.where(mine, held, flipped(held, "dp", 1))
    share = jnp.where(core == 0, held[: channels + 8], jnp.pad(held[channels + 8 :], ((0, 8), (0, 0))))
    always = lambda at, lev: True
    turn = lambda value, step: routed(value, always, lambda at, lev: (at ^ (2 << (core_of(at) ^ step)), lev))
    one = turn(share, 0)
    two = turn(share, 1)
    three = turn(one, 1)
    shares = jnp.stack([share, jnp.where(core == 0, one, two), jnp.where(core == 0, two, one), three])
    others = flipped(shares, "dp", 1)
    in_shares = jnp.where(core == 0, shares, others)
    out_shares = jnp.where(core == 0, others, shares)
    ordered_in = [picked(in_shares, quarter ^ c) for c in range(PARTS)]
    ordered_out = [picked(out_shares, quarter ^ c)[:channels] for c in range(PARTS)]
    grad_weight_in = jnp.concatenate([value[:channels] for value in ordered_in]).astype(F32)
    grad_weight_out = jnp.concatenate(ordered_out).astype(F32).T
    grad_bias_in = ordered_in[0][channels].astype(F32)
    return (
        output,
        grad_inputs,
        small[:49].reshape(7, 7, channels),
        small[49],
        small[50],
        small[51],
        grad_weight_in,
        grad_bias_in,
        grad_weight_out,
        small[52],
    )


def solution(mesh):
    in_specs = (
        P("dp", None, "chan"),
        P("dp", None),
        P(),
        P(None, None, "chan"),
        P("chan"),
        P("chan"),
        P("chan"),
        P(None, "chan"),
        P("chan"),
        P("chan", None),
        P("chan"),
        P("dp", None, "chan"),
    )
    out_specs = (
        P("dp", None, "chan"),
        P("dp", None, "chan"),
        P(None, None, "chan"),
        P("chan"),
        P("chan"),
        P("chan"),
        P(None, "chan"),
        P("chan"),
        P("chan", None),
        P("chan"),
    )
    return jax.shard_map(body, mesh=mesh, in_specs=in_specs, out_specs=out_specs, check_vma=False)
```

time: 979 us -> 490 us (0.50)
  waiting for transfers between devices: 539 us -> 186 us
  other arithmetic: 269 us -> 31.8 us
  Pallas kernels: 0 us -> 122 us
  starting transfers between devices: 1.81 us -> 102 us
  matrix products: 91.5 us -> 0 us
  blocking collectives: 26.5 us -> 0 us
  local copies, waits for them, and re-layouts: 27.8 us -> 45.3 us
  between operations: 15.8 us -> 1.41 us
    unnamed x7 -> x0, waiting for transfers between devices: 355 us -> none
    ppermute x5 -> x53, waiting for transfers between devices: 1.99 us -> 186 us  [the longest x41 127 us: flipped(): lax.ppermute(block, axis, [(place, place ^ bit) for place in range(count)])]
    all_gather x2 -> x0, waiting for transfers between devices: 182 us -> none  [the longest x1 108 us: body(): gathered = lax.all_gather(normed, 'chan', axis=1, tiled=True)]
    reduce_sum x14 -> x1, other arithmetic: 173 us -> 0.63 us  [body(): jnp.sum(jnp.where(jnp.arange(counts.shape[0]) == sample, counts, 0))]
    pallas_call x0 -> x8, Pallas kernels: none -> 122 us  [the longest x1 56 us: pointwise(): pl.pallas_call(pointwise_kernel, grid=(win.shape[2] // TILE,), out_shape=...]
    ppermute x5 -> x53, starting transfers between devices: 0.96 us -> 102 us  [the longest x41 54.1 us: flipped(): lax.ppermute(block, axis, [(place, place ^ bit) for place in range(count)])]
    dot_general x6 -> x0, matrix products: 91.5 us -> none  [the longest x1 35.8 us: body(): jnp.dot(gathered, weight_in, preferred_element_type=jnp.float32) + bias_in]
    mul x3 -> x0, other arithmetic: 78.6 us -> none  [the longest x1 78.5 us: body(): grad_inputs = wet_cells * history_keep * (grad_res + grad_masked)]
  transfers between devices with their start and end apart: 10 -> 53, of which waited for: 6 -> 21; matrix products, arithmetic and copies ran while one was open for 27% -> 9% of each run, Pallas kernels for 0% -> 13%
where the time goes in v1:
time: 490 us; the launch traced here: 489 us
  waiting for transfers between devices  186 us (38%)
  Pallas kernels  122 us (25%)
  starting transfers between devices  102 us (21%)
  local copies, waits for them, and re-layouts  45.3 us (9%)
  other arithmetic  31.8 us (6%)
    ppermute x41, waiting for transfers between devices, flipped(): lax.ppermute(block, axis, [(place, place ^ bit) for place in range(count)])  127 us
    ppermute x12, waiting for transfers between devices, routed(): return lax.ppermute(block, ('dp', 'chan'), route)  58.9 us
    pallas_call x1, Pallas kernels, pointwise(): pl.pallas_call(pointwise_kernel, grid=(win.shape[2] // TILE,), out_shape=...  56 us
    ppermute x41, starting transfers between devices, flipped(): lax.ppermute(block, axis, [(place, place ^ bit) for place in range(count)])  54.1 us
    ppermute x12, starting transfers between devices, routed(): return lax.ppermute(block, ('dp', 'chan'), route)  47.9 us
    pallas_call x1, Pallas kernels, depthwise_back(): pl.pallas_call(depthwise_back_kernel, out_shape=(jax.ShapeDtypeStruct(x.s...  31.6 us
    unnamed x110, local copies, waits for them, and re-layouts  30 us
    pallas_call x1, Pallas kernels, depthwise(): pl.pallas_call(depthwise_kernel, out_shape=(jax.ShapeDtypeStruct(x.shape,...  23 us
  transfers between devices with their start and end apart: 53, of which 21 were waited for; matrix products, arithmetic and copies ran while one was open for 9% of the time, Pallas kernels for 13%

profile of v1, /device:TPU:0, one launch (start us, length us, event | category | flops | bytes accessed | tf_op | source)
XLA Modules:
  0.0 488.6 jit_solution(17582329741984736984)
XLA Ops:
  5.1 6.8 %collective-permute-start.16 = (bf16[2,200,800]{2,1,0:T(8,128)(2,1)}, bf16[2,200,800]{2,1,0:T(8,128)(2,1)}, u32[]{:S(2)}, u32[]{:S(2)}) collective-permute-start(bf16[2,200,800]{2,1,0:T(8,128)(2,1)} %pad_maximum_fusion.2), channel_id=1, source_target_pairs={{0,2},{1,3},{6,4},{7,5},{8,10},{9,11},{14,12},{15,13},{16,18},{17,... | collective-permute-start | bytes 1920008 | tf_op jit(solution)/shard_map/ppermute | solution.py:36
  25.9 16.9 %collective-permute-done.17 = bf16[2,200,800]{2,1,0:T(8,128)(2,1)} collective-permute-done((bf16[2,200,800]{2,1,0:T(8,128)(2,1)}, bf16[2,200,800]{2,1,0:T(8,128)(2,1)}, u32[]{:S(2)}, u32[]{:S(2)}) %collective-permute-start.17) | collective-permute-done | bytes 640032 | tf_op jit(solution)/shard_map/ppermute | solution.py:36
  54.2 14.0 %collective-permute-start.26 = (f32[1,800]{1,0:T(1,128)S(1)}, f32[1,800]{1,0:T(1,128)S(1)}, u32[]{:S(2)}, u32[]{:S(2)}) collective-permute-start(f32[1,800]{1,0:T(1,128)S(1)} %reshape.172), channel_id=1, source_target_pairs={{0,1},{1,0},{6,7},{7,6},{8,9},{9,8},{14,15},{15,14},{16,17},{17,16... | collective-permute-start | bytes 9608 | tf_op jit(solution)/shard_map/ppermute | solution.py:36
  74.4 23.0 %depthwise.1 = (f32[24,152,200]{2,1,0:T(8,128)S(1)}, f32[2,200]{1,0:T(2,128)S(1)}) custom-call(s32[1]{0:T(128)} %bitcast.4.within_ref, bf16[24,152,200]{2,1,0:T(8,128)(2,1)S(1)} %copy-done.8, bf16[3,152,200]{2,1,0:T(8,128)(2,1)S(1)} %collective-permute-done.rim_ref, f32[24,152,1]{2,1,0:T(8,128)S(1)} %copy.40.wet_ref, ...), custom_call_target="tpu_custom_call" | custom-call | flops 71500800 | bytes 4377600 | tf_op jit(solution)/shard_map/depthwise/pallas_call | solution.py:118
  108.4 6.1 %collective-permute-done.11.refs_11_ = bf16[912,200]{1,0:T(8,128)(2,1)} collective-permute-done((bf16[912,200]{1,0:T(8,128)(2,1)S(1)}, bf16[912,200]{1,0:T(8,128)(2,1)}, u32[]{:S(2)}, u32[]{:S(2)}) %collective-permute-start.11) | collective-permute-done | bytes 364832 | tf_op jit(solution)/shard_map/ppermute | solution.py:25
  114.5 9.6 %collective-permute-start.2 = (bf16[912,200]{1,0:T(8,128)(2,1)S(1)}, bf16[912,200]{1,0:T(8,128)(2,1)S(1)}, u32[]{:S(2)}, u32[]{:S(2)}) collective-permute-start(bf16[912,200]{1,0:T(8,128)(2,1)S(1)} %get-tuple-element.38), channel_id=1, source_target_pairs={{0,1},{1,0},{2,3},{3,2},{4,5},{5,4},{6,7},{7,6},{8,9},{9,8},{10,11... | collective-permute-start | bytes 1094408 | tf_op jit(solution)/shard_map/ppermute | solution.py:25
  126.0 18.6 %collective-permute-done.2.refs_1_ = bf16[912,200]{1,0:T(8,128)(2,1)S(1)} collective-permute-done((bf16[912,200]{1,0:T(8,128)(2,1)S(1)}, bf16[912,200]{1,0:T(8,128)(2,1)S(1)}, u32[]{:S(2)}, u32[]{:S(2)}) %collective-permute-start.2) | collective-permute-done | bytes 364832 | tf_op jit(solution)/shard_map/ppermute | solution.py:25
  152.0 6.0 %collective-permute-done.4.refs_3_ = bf16[912,200]{1,0:T(8,128)(2,1)S(1)} collective-permute-done((bf16[912,200]{1,0:T(8,128)(2,1)S(1)}, bf16[912,200]{1,0:T(8,128)(2,1)S(1)}, u32[]{:S(2)}, u32[]{:S(2)}) %collective-permute-start.4) | collective-permute-done | bytes 364832 | tf_op jit(solution)/shard_map/ppermute | solution.py:25
  158.6 5.4 %collective-permute-done.20 = bf16[200,1600]{1,0:T(8,128)(2,1)S(1)} collective-permute-done((bf16[200,1600]{1,0:T(8,128)(2,1)S(1)}, bf16[200,1600]{1,0:T(8,128)(2,1)S(1)}, u32[]{:S(2)}, u32[]{:S(2)}) %collective-permute-start.20) | collective-permute-done | bytes 640032 | tf_op jit(solution)/shard_map/ppermute | solution.py:25
  164.1 13.4 %collective-permute-done.21 = bf16[200,1600]{1,0:T(8,128)(2,1)S(1)} collective-permute-done((bf16[200,1600]{1,0:T(8,128)(2,1)S(1)}, bf16[200,1600]{1,0:T(8,128)(2,1)S(1)}, u32[]{:S(2)}, u32[]{:S(2)}) %collective-permute-start.21) | collective-permute-done | bytes 640032 | tf_op jit(solution)/shard_map/ppermute | solution.py:25
  181.9 56.0 %pointwise.1 = (bf16[4,912,200]{2,1,0:T(8,128)(2,1)}, bf16[4,912,200]{2,1,0:T(8,128)(2,1)}, bf16[4,912,200]{2,1,0:T(8,128)(2,1)}, bf16[4,912,200]{2,1,0:T(8,128)...) custom-call(s32[1]{0:T(128)} %bitcast.3.twist_ref, ...), custom_call_target="tpu_custom_call" | custom-call | flops 28016640000 | bytes 41943040 | tf_op jit(solution)/shard_map/pointwise/pallas_call | solution.py:459
  240.0 29.9 %collective-permute-done.43 = bf16[2,200,1600]{2,1,0:T(8,128)(2,1)S(1)} collective-permute-done((bf16[2,200,1600]{2,1,0:T(8,128)(2,1)}, bf16[2,200,1600]{2,1,0:T(8,128)(2,1)S(1)}, u32[]{:S(2)}, u32[]{:S(2)}) %collective-permute-start.43) | collective-permute-done | bytes 1280032 | tf_op jit(solution)/shard_map/ppermute | solution.py:25
  274.6 14.1 %collective-permute-done.44 = bf16[200,1600]{1,0:T(8,128)(2,1)S(1)} collective-permute-done((bf16[200,1600]{1,0:T(8,128)(2,1)S(1)}, bf16[200,1600]{1,0:T(8,128)(2,1)S(1)}, u32[]{:S(2)}, u32[]{:S(2)}) %collective-permute-start.44) | collective-permute-done | bytes 640032 | tf_op jit(solution)/shard_map/ppermute | solution.py:25
  291.6 14.6 %collective-permute-start.45 = (bf16[408,800]{1,0:T(8,128)(2,1)S(1)}, bf16[408,800]{1,0:T(8,128)(2,1)S(1)}, u32[]{:S(2)}, u32[]{:S(2)}) collective-permute-start(bf16[408,800]{1,0:T(8,128)(2,1)S(1)} %get-tuple-element.119), channel_id=1, source_target_pairs={{0,1},{1,0},{6,7},{7,6},{8,9},{9,8},{14,15},{15,14},{16,17},{17,16... | collective-permute-start | bytes 1958408 | tf_op jit(solution)/shard_map/ppermute | solution.py:36
  308.8 11.4 %collective-permute-done.45 = bf16[408,800]{1,0:T(8,128)(2,1)S(1)} collective-permute-done((bf16[408,800]{1,0:T(8,128)(2,1)S(1)}, bf16[408,800]{1,0:T(8,128)(2,1)S(1)}, u32[]{:S(2)}, u32[]{:S(2)}) %collective-permute-start.45) | collective-permute-done | bytes 652832 | tf_op jit(solution)/shard_map/ppermute | solution.py:36
  320.3 15.6 %collective-permute-done.46 = bf16[408,800]{1,0:T(8,128)(2,1)S(1)} collective-permute-done((bf16[408,800]{1,0:T(8,128)(2,1)S(1)}, bf16[408,800]{1,0:T(8,128)(2,1)S(1)}, u32[]{:S(2)}, u32[]{:S(2)}) %collective-permute-start.46) | collective-permute-done | bytes 652832 | tf_op jit(solution)/shard_map/ppermute | solution.py:36
  336.3 4.0 copy.41
  344.5 10.2 %collective-permute-done.49 = bf16[208,800]{1,0:T(8,128)(2,1)} collective-permute-done((bf16[208,800]{1,0:T(8,128)(2,1)S(1)}, bf16[208,800]{1,0:T(8,128)(2,1)}, u32[]{:S(2)}, u32[]{:S(2)}) %collective-permute-start.49) | collective-permute-done | bytes 332832 | tf_op jit(solution)/shard_map/ppermute | solution.py:36
  366.4 8.4 %collective-permute-start.33 = (bf16[912,200]{1,0:T(8,128)(2,1)}, bf16[912,200]{1,0:T(8,128)(2,1)S(1)}, u32[]{:S(2)}, u32[]{:S(2)}) collective-permute-start(bf16[912,200]{1,0:T(8,128)(2,1)} %get-tuple-element.94), channel_id=1, source_target_pairs={{0,1},{1,0},{2,3},{3,2},{4,5},{5,4},{6,7},{7,6},{8,9},{9,8},{10,11... | collective-permute-start | bytes 1094408 | tf_op jit(solution)/shard_map/ppermute | solution.py:25
  385.0 10.3 %collective-permute-done.33.refs_1_ = bf16[912,200]{1,0:T(8,128)(2,1)S(1)} collective-permute-done((bf16[912,200]{1,0:T(8,128)(2,1)}, bf16[912,200]{1,0:T(8,128)(2,1)S(1)}, u32[]{:S(2)}, u32[]{:S(2)}) %collective-permute-start.33) | collective-permute-done | bytes 364832 | tf_op jit(solution)/shard_map/ppermute | solution.py:25
  395.4 14.2 %collective-permute-done.34.refs_2_ = bf16[912,200]{1,0:T(8,128)(2,1)S(1)} collective-permute-done((bf16[912,200]{1,0:T(8,128)(2,1)}, bf16[912,200]{1,0:T(8,128)(2,1)S(1)}, u32[]{:S(2)}, u32[]{:S(2)}) %collective-permute-start.34) | collective-permute-done | bytes 364832 | tf_op jit(solution)/shard_map/ppermute | solution.py:25
  414.8 9.8 %collective-permute-start.29 = (bf16[912,200]{1,0:T(8,128)(2,1)}, bf16[912,200]{1,0:T(8,128)(2,1)S(1)}, u32[]{:S(2)}, u32[]{:S(2)}) collective-permute-start(bf16[912,200]{1,0:T(8,128)(2,1)} %get-tuple-element.98), channel_id=1, source_target_pairs={{0,1},{1,0},{2,3},{3,2},{4,5},{5,4},{6,7},{7,6},{8,9},{9,8},{10,11... | collective-permute-start | bytes 1094408 | tf_op jit(solution)/shard_map/ppermute | solution.py:25
  431.8 31.6 %depthwise_back.1 = (f32[24,152,200]{2,1,0:T(8,128)}, f32[49,200]{1,0:T(8,128)S(1)}) custom-call(s32[1]{0:T(128)} %bitcast.4.within_ref, f32[24,152,200]{2,1,0:T(8,128)} %copy-done.13, bf16[3,152,200]{2,1,0:T(8,128)(2,1)S(1)} %collective-permute-done.37.rim_ref, bf16[24,152,200]{2,1,0:T(8,128)(2,1)S(1)} %copy-done.9, bf16[24,152,200]{2,1,0:T(8,128)(2,1)S(1)} %copy-done.12, ...), custom_call_target="tpu_custom_call" | custom-call | flops 143001600 | bytes 8755200 | tf_op jit(solution)/shard_map/depthwise_back/pallas_call | solution.py:181
  471.8 4.5 finish.1
  (257 shorter events, 132.7 us)
Async XLA Ops:
  11.9 30.9 %collective-permute-start.17 = (bf16[2,200,800]{2,1,0:T(8,128)(2,1)}, bf16[2,200,800]{2,1,0:T(8,128)(2,1)}, u32[]{:S(2)}, u32[]{:S(2)}) collective-permute-start(bf16[2,200,800]{2,1,0:T(8,128)(2,1)} %pad_maximum_fusion.2), channel_id=1, source_target_pairs={{0,1},{1,0},{6,7},{7,6},{8,9},{9,8},{14,15},{15,14},{16,17},{17,16... | collective-permute-start | bytes 1920008 | tf_op jit(solution)/shard_map/ppermute | solution.py:36
  15.4 30.2 %collective-permute-start.18 = (bf16[2,200,800]{2,1,0:T(8,128)(2,1)}, bf16[2,200,800]{2,1,0:T(8,128)(2,1)}, u32[]{:S(2)}, u32[]{:S(2)}) collective-permute-start(bf16[2,200,800]{2,1,0:T(8,128)(2,1)} %pad_maximum_fusion.2), channel_id=1, source_target_pairs={{0,3},{1,2},{6,5},{7,4},{8,11},{9,10},{14,13},{15,12},{16,19},{17,... | collective-permute-start | bytes 1920008 | tf_op jit(solution)/shard_map/ppermute | solution.py:36
  23.7 78.2 %collective-permute-start.9 = (bf16[912,200]{1,0:T(8,128)(2,1)}, bf16[912,200]{1,0:T(8,128)(2,1)}, u32[]{:S(2)}, u32[]{:S(2)}) collective-permute-start(bf16[912,200]{1,0:T(8,128)(2,1)} %get-tuple-element.42), channel_id=1, source_target_pairs={{0,1},{1,0},{2,3},{3,2},{4,5},{5,4},{6,7},{7,6},{8,9},{9,8},{10,11... | collective-permute-start | bytes 1094408 | tf_op jit(solution)/shard_map/ppermute | solution.py:25
  24.1 79.3 %collective-permute-start.10 = (bf16[912,200]{1,0:T(8,128)(2,1)}, bf16[912,200]{1,0:T(8,128)(2,1)}, u32[]{:S(2)}, u32[]{:S(2)}) collective-permute-start(bf16[912,200]{1,0:T(8,128)(2,1)} %get-tuple-element.43), channel_id=1, source_target_pairs={{0,2},{1,3},{2,0},{3,1},{4,6},{5,7},{6,4},{7,5},{8,10},{9,11},{10,... | collective-permute-start | bytes 1094408 | tf_op jit(solution)/shard_map/ppermute | solution.py:25
  48.2 55.7 %collective-permute-start.23 = (bf16[200,1600]{1,0:T(8,128)(2,1)}, bf16[200,1600]{1,0:T(8,128)(2,1)}, u32[]{:S(2)}, u32[]{:S(2)}) collective-permute-start(bf16[200,1600]{1,0:T(8,128)(2,1)} %bitcast.17), channel_id=1, source_target_pairs={{0,16},{4,20},{8,24},{12,28},{16,0},{20,4},{24,8},{28,12},{1,17},{... | collective-permute-start | bytes 1920008 | tf_op jit(solution)/shard_map/ppermute | solution.py:25
  69.8 29.5 %collective-permute-start.27 = (f32[1,800]{1,0:T(1,128)S(1)}, f32[1,800]{1,0:T(1,128)S(1)}, u32[]{:S(2)}, u32[]{:S(2)}) collective-permute-start(f32[1,800]{1,0:T(1,128)S(1)} %reshape.172), channel_id=1, source_target_pairs={{0,3},{1,2},{6,5},{7,4},{8,11},{9,10},{14,13},{15,12},{16,19},{17,... | collective-permute-start | bytes 9608 | tf_op jit(solution)/shard_map/ppermute | solution.py:36
  101.8 43.9 %collective-permute-start.22 = (bf16[200,1600]{1,0:T(8,128)(2,1)}, bf16[200,1600]{1,0:T(8,128)(2,1)S(1)}, u32[]{:S(2)}, u32[]{:S(2)}) collective-permute-start(bf16[200,1600]{1,0:T(8,128)(2,1)} %bitcast.17), channel_id=1, source_target_pairs={{0,8},{4,12},{8,0},{12,4},{16,24},{20,28},{24,16},{28,20},{1,9},{5... | collective-permute-start | bytes 1920008 | tf_op jit(solution)/shard_map/ppermute | solution.py:25
  103.4 42.9 %collective-permute-start.19 = (bf16[200,1600]{1,0:T(8,128)(2,1)}, bf16[200,1600]{1,0:T(8,128)(2,1)S(1)}, u32[]{:S(2)}, u32[]{:S(2)}) collective-permute-start(bf16[200,1600]{1,0:T(8,128)(2,1)} %bitcast.94), channel_id=1, source_target_pairs={{0,8},{4,12},{8,0},{12,4},{16,24},{20,28},{24,16},{28,20},{1,9},{5... | collective-permute-start | bytes 1920008 | tf_op jit(solution)/shard_map/ppermute | solution.py:25
  103.9 44.0 %collective-permute-start.24 = (bf16[200,1600]{1,0:T(8,128)(2,1)}, bf16[200,1600]{1,0:T(8,128)(2,1)S(1)}, u32[]{:S(2)}, u32[]{:S(2)}) collective-permute-start(bf16[200,1600]{1,0:T(8,128)(2,1)} %collective-permute-done.23), channel_id=1, source_target_pairs={{0,8},{4,12},{8,0},{12,4},{16,24},{20,28},{24,16},{28,20},{1,9},{5... | collective-permute-start | bytes 1920008 | tf_op jit(solution)/shard_map/ppermute | solution.py:25
  114.5 30.0 %collective-permute-start.2 = (bf16[912,200]{1,0:T(8,128)(2,1)S(1)}, bf16[912,200]{1,0:T(8,128)(2,1)S(1)}, u32[]{:S(2)}, u32[]{:S(2)}) collective-permute-start(bf16[912,200]{1,0:T(8,128)(2,1)S(1)} %get-tuple-element.38), channel_id=1, source_target_pairs={{0,1},{1,0},{2,3},{3,2},{4,5},{5,4},{6,7},{7,6},{8,9},{9,8},{10,11... | collective-permute-start | bytes 1094408 | tf_op jit(solution)/shard_map/ppermute | solution.py:25
  147.9 29.5 %collective-permute-start.21 = (bf16[200,1600]{1,0:T(8,128)(2,1)S(1)}, bf16[200,1600]{1,0:T(8,128)(2,1)S(1)}, u32[]{:S(2)}, u32[]{:S(2)}) collective-permute-start(bf16[200,1600]{1,0:T(8,128)(2,1)S(1)} %collective-permute-done.19), channel_id=1, source_target_pairs={{0,16},{4,20},{8,24},{12,28},{16,0},{20,4},{24,8},{28,12},{1,17},{... | collective-permute-start | bytes 1920008 | tf_op jit(solution)/shard_map/ppermute | solution.py:25
  237.9 31.9 %collective-permute-start.43 = (bf16[2,200,1600]{2,1,0:T(8,128)(2,1)}, bf16[2,200,1600]{2,1,0:T(8,128)(2,1)S(1)}, u32[]{:S(2)}, u32[]{:S(2)}) collective-permute-start(bf16[2,200,1600]{2,1,0:T(8,128)(2,1)} %get-tuple-element.59), channel_id=1, source_target_pairs={{0,16},{4,20},{8,24},{12,28},{16,0},{20,4},{24,8},{28,12},{1,17},{... | collective-permute-start | bytes 3840008 | tf_op jit(solution)/shard_map/ppermute | solution.py:25
  238.6 35.1 %collective-permute-start.41 = (bf16[2,208,1600]{2,1,0:T(8,128)(2,1)}, bf16[2,208,1600]{2,1,0:T(8,128)(2,1)S(1)}, u32[]{:S(2)}, u32[]{:S(2)}) collective-permute-start(bf16[2,208,1600]{2,1,0:T(8,128)(2,1)} %get-tuple-element.57), channel_id=1, source_target_pairs={{0,8},{4,12},{8,0},{12,4},{16,24},{20,28},{24,16},{28,20},{1,9},{5... | collective-permute-start | bytes 3993608 | tf_op jit(solution)/shard_map/ppermute | solution.py:25
  291.6 28.7 %collective-permute-start.45 = (bf16[408,800]{1,0:T(8,128)(2,1)S(1)}, bf16[408,800]{1,0:T(8,128)(2,1)S(1)}, u32[]{:S(2)}, u32[]{:S(2)}) collective-permute-start(bf16[408,800]{1,0:T(8,128)(2,1)S(1)} %get-tuple-element.119), channel_id=1, source_target_pairs={{0,1},{1,0},{6,7},{7,6},{8,9},{9,8},{14,15},{15,14},{16,17},{17,16... | collective-permute-start | bytes 1958408 | tf_op jit(solution)/shard_map/ppermute | solution.py:36
  306.2 29.6 %collective-permute-start.46 = (bf16[408,800]{1,0:T(8,128)(2,1)S(1)}, bf16[408,800]{1,0:T(8,128)(2,1)S(1)}, u32[]{:S(2)}, u32[]{:S(2)}) collective-permute-start(bf16[408,800]{1,0:T(8,128)(2,1)S(1)} %get-tuple-element.118), channel_id=1, source_target_pairs={{2,0},{3,1},{4,6},{5,7},{10,8},{11,9},{12,14},{13,15},{18,16},{19,... | collective-permute-start | bytes 1958408 | tf_op jit(solution)/shard_map/ppermute | solution.py:36
  307.5 28.3 %collective-permute-start.47 = (bf16[408,800]{1,0:T(8,128)(2,1)S(1)}, bf16[408,800]{1,0:T(8,128)(2,1)S(1)}, u32[]{:S(2)}, u32[]{:S(2)}) collective-permute-start(bf16[408,800]{1,0:T(8,128)(2,1)S(1)} %get-tuple-element.119), channel_id=1, source_target_pairs={{2,1},{3,0},{4,7},{5,6},{10,9},{11,8},{12,15},{13,14},{18,17},{19,... | collective-permute-start | bytes 1958408 | tf_op jit(solution)/shard_map/ppermute | solution.py:36
  342.7 34.5 %collective-permute-start.28 = (bf16[4,912,200]{1,2,0:T(8,128)(2,1)}, bf16[4,912,200]{1,2,0:T(8,128)(2,1)}, u32[]{:S(2)}, u32[]{:S(2)}) collective-permute-start(bf16[4,912,200]{1,2,0:T(8,128)(2,1)} %copy.35), channel_id=1, source_target_pairs={{0,4},{4,0},{8,12},{12,8},{16,20},{20,16},{24,28},{28,24},{1,5},{5... | collective-permute-start | bytes 4377608 | tf_op jit(solution)/shard_map/ppermute | solution.py:25
  364.9 112.5 %collective-permute-start.52 = (bf16[4,208,800]{2,1,0:T(8,128)(2,1)}, bf16[4,208,800]{2,1,0:T(8,128)(2,1)}, u32[]{:S(2)}, u32[]{:S(2)}) collective-permute-start(bf16[4,208,800]{2,1,0:T(8,128)(2,1)} %pad_maximum_fusion.1), channel_id=1, source_target_pairs={{0,4},{4,0},{8,12},{12,8},{16,20},{20,16},{24,28},{28,24},{1,5},{5... | collective-permute-start | bytes 3993608 | tf_op jit(solution)/shard_map/ppermute | solution.py:25
  366.4 28.9 %collective-permute-start.33 = (bf16[912,200]{1,0:T(8,128)(2,1)}, bf16[912,200]{1,0:T(8,128)(2,1)S(1)}, u32[]{:S(2)}, u32[]{:S(2)}) collective-permute-start(bf16[912,200]{1,0:T(8,128)(2,1)} %get-tuple-element.94), channel_id=1, source_target_pairs={{0,1},{1,0},{2,3},{3,2},{4,5},{5,4},{6,7},{7,6},{8,9},{9,8},{10,11... | collective-permute-start | bytes 1094408 | tf_op jit(solution)/shard_map/ppermute | solution.py:25
  374.8 34.7 %collective-permute-start.34 = (bf16[912,200]{1,0:T(8,128)(2,1)}, bf16[912,200]{1,0:T(8,128)(2,1)S(1)}, u32[]{:S(2)}, u32[]{:S(2)}) collective-permute-start(bf16[912,200]{1,0:T(8,128)(2,1)} %get-tuple-element.93), channel_id=1, source_target_pairs={{0,2},{1,3},{2,0},{3,1},{4,6},{5,7},{6,4},{7,5},{8,10},{9,11},{10,... | collective-permute-start | bytes 1094408 | tf_op jit(solution)/shard_map/ppermute | solution.py:25
  374.9 34.6 %collective-permute-start.35 = (bf16[912,200]{1,0:T(8,128)(2,1)}, bf16[912,200]{1,0:T(8,128)(2,1)S(1)}, u32[]{:S(2)}, u32[]{:S(2)}) collective-permute-start(bf16[912,200]{1,0:T(8,128)(2,1)} %get-tuple-element.92), channel_id=1, source_target_pairs={{0,3},{1,2},{2,1},{3,0},{4,7},{5,6},{6,5},{7,4},{8,11},{9,10},{10,... | collective-permute-start | bytes 1094408 | tf_op jit(solution)/shard_map/ppermute | solution.py:25
  414.8 55.4 %collective-permute-start.29 = (bf16[912,200]{1,0:T(8,128)(2,1)}, bf16[912,200]{1,0:T(8,128)(2,1)S(1)}, u32[]{:S(2)}, u32[]{:S(2)}) collective-permute-start(bf16[912,200]{1,0:T(8,128)(2,1)} %get-tuple-element.98), channel_id=1, source_target_pairs={{0,1},{1,0},{2,3},{3,2},{4,5},{5,4},{6,7},{7,6},{8,9},{9,8},{10,11... | collective-permute-start | bytes 1094408 | tf_op jit(solution)/shard_map/ppermute | solution.py:25
  424.6 45.6 %collective-permute-start.30 = (bf16[912,200]{1,0:T(8,128)(2,1)}, bf16[912,200]{1,0:T(8,128)(2,1)S(1)}, u32[]{:S(2)}, u32[]{:S(2)}) collective-permute-start(bf16[912,200]{1,0:T(8,128)(2,1)} %get-tuple-element.97), channel_id=1, source_target_pairs={{0,2},{1,3},{2,0},{3,1},{4,6},{5,7},{6,4},{7,5},{8,10},{9,11},{10,... | collective-permute-start | bytes 1094408 | tf_op jit(solution)/shard_map/ppermute | solution.py:25
  424.7 45.5 %collective-permute-start.31 = (bf16[912,200]{1,0:T(8,128)(2,1)}, bf16[912,200]{1,0:T(8,128)(2,1)}, u32[]{:S(2)}, u32[]{:S(2)}) collective-permute-start(bf16[912,200]{1,0:T(8,128)(2,1)} %get-tuple-element.96), channel_id=1, source_target_pairs={{0,3},{1,2},{2,1},{3,0},{4,7},{5,6},{6,5},{7,4},{8,11},{9,10},{10,... | collective-permute-start | bytes 1094408 | tf_op jit(solution)/shard_map/ppermute | solution.py:25
  (79 other events, 1068.5 us)

commit v2 on v1

--- a/solution.py
+++ b/solution.py
@@ -381,50 +381,118 @@
     )(level, x, wet, keep, bias, *blocks)
 
 
-def pointwise_kernel(twist_ref, *refs):
-    acts = refs[: 4 * PARTS]
-    win_ref, wout_ref, bias_ref = refs[4 * PARTS : 4 * PARTS + 3]
-    outs = refs[4 * PARTS + 3 : 4 * PARTS + 11]
-    grad_own_ref, grad_far_ref, own_ref, far_ref, in_keep_ref, in_send_ref, out_keep_ref, out_send_ref = outs
-    turned_ref, turned_grad_ref, back_ref, branch_ref, hidden_ref, slope_ref, active_ref, grad_hidden_ref = refs[
-        4 * PARTS + 11 :
+TURNED = (((1,), (1,)), ((), ()))
+
+
+def forward_kernel(twist_ref, *refs):
+    acts = refs[: 2 * PARTS]
+    win_ref, wout_ref, bias_ref, own_ref, far_ref, active_ref, slope_ref, turned_ref, branch_ref, hidden_ref = refs[
+        2 * PARTS :
     ]
     twist = twist_ref[0]
     cells, channels = acts[0].shape
-    normed = (acts[:PARTS], acts[PARTS : 2 * PARTS])
-    grads = (acts[2 * PARTS : 3 * PARTS], acts[3 * PARTS :])
 
     @pl.when(pl.program_id(0) == 0)
     def _():
         for side in range(2):
             for k in range(PARTS):
-                turned_ref[side, k, 0:channels, :] = normed[side][k][...].T
+                turned_ref[side, k, 0:channels, :] = acts[side * PARTS + k][...].T
                 ones = (lax.broadcasted_iota(jnp.int32, (8, cells), 0) == 0).astype(BF16)
                 turned_ref[side, k, channels : channels + 8, :] = ones
-                turned_grad_ref[side, k] = grads[side][k][...].T
-        back_ref[...] = jnp.zeros_like(back_ref)
         branch_ref[...] = jnp.zeros_like(branch_ref)
 
     for side in range(2):
         hidden = jnp.broadcast_to(bias_ref[...], (cells, TILE))
-        grad = jnp.zeros((cells, TILE), F32)
         for k in range(PARTS):
-            hidden = hidden + jnp.dot(normed[side][k][...], win_ref[twist ^ k], preferred_element_type=F32)
-            grad = grad + jnp.dot(grads[side][k][...], wout_ref[twist ^ k], preferred_element_type=F32)
+            hidden = hidden + jnp.dot(
+                acts[side * PARTS + k][...], win_ref[twist ^ k], preferred_element_type=F32
+            )
         hidden_ref[side] = hidden
-        slope_ref[side] = grad
         value = hidden_ref[side]
         cumulative = 0.5 * (1.0 + lax.erf(value * 0.7071067811865476))
         density = jnp.exp(-0.5 * value * value) * 0.3989422804014327
         active_ref[side] = (value * cumulative).astype(BF16)
-        grad_hidden_ref[side] = (slope_ref[side] * (cumulative + value * density)).astype(BF16)
-        dims = (((1,), (1,)), ((), ()))
+        slope_ref[side] = cumulative + value * density
         for k in range(PARTS):
             branch_ref[side, k] += lax.dot_general(
-                active_ref[side], wout_ref[twist ^ k], dims, preferred_element_type=F32
+                active_ref[side], wout_ref[twist ^ k], TURNED, preferred_element_type=F32
             )
+
+    @pl.when(pl.program_id(0) == pl.num_programs(0) - 1)
+    def _():
+        own_ref[...] = branch_ref[0].astype(BF16)
+        far_ref[...] = branch_ref[1].astype(BF16)
+
+
+def whole(*shape):
+    return pl.BlockSpec(shape, lambda t: (0,) * len(shape), pipeline_mode=pl.Buffered(1))
+
+
+def tiled(*shape):
+    return pl.BlockSpec(shape + (TILE,), lambda t: (0,) * len(shape) + (t,))
+
+
+def forward(twist, acts, win, wout, bias):
+    cells, channels = acts[0].shape
+    units = win.shape[2]
+    quad = jax.ShapeDtypeStruct((PARTS, cells, channels), BF16)
+    return pl.pallas_call(
+        forward_kernel,
+        grid=(units // TILE,),
+        out_shape=(
+            quad,
+            quad,
+            jax.ShapeDtypeStruct((2, cells, units), BF16),
+            jax.ShapeDtypeStruct((2, cells, units), F32),
+            jax.ShapeDtypeStruct((2, PARTS, channels + 8, cells), BF16),
+        ),
+        in_specs=[SMEM]
+        + [whole(cells, channels)] * (2 * PARTS)
+        + [tiled(PARTS, channels), tiled(PARTS, channels), tiled(1)],
+        out_specs=(
+            whole(PARTS, cells, channels),
+            whole(PARTS, cells, channels),
+            tiled(2, cells),
+            tiled(2, cells),
+            whole(2, PARTS, channels + 8, cells),
+        ),
+        scratch_shapes=[
+            pltpu.VMEM((2, PARTS, cells, channels), F32),
+            pltpu.VMEM((2, cells, TILE), F32),
+        ],
+        compiler_params=pltpu.CompilerParams(vmem_limit_bytes=60 << 20, dimension_semantics=("arbitrary",)),
+        cost_estimate=pl.CostEstimate(
+            flops=8 * cells * PARTS * channels * units, bytes_accessed=32 << 20, transcendentals=4 * cells * units
+        ),
+        name="forward",
+    )(twist, *acts, win, wout, bias)
+
+
+def backward_kernel(twist_ref, *refs):
+    grads = refs[: 2 * PARTS]
+    turned_ref, win_ref, wout_ref, active_ref, slope_ref = refs[2 * PARTS : 2 * PARTS + 5]
+    own_ref, far_ref, in_keep_ref, in_send_ref, out_keep_ref, out_send_ref = refs[2 * PARTS + 5 : 2 * PARTS + 11]
+    turned_grad_ref, back_ref, grad_hidden_ref = refs[2 * PARTS + 11 :]
+    twist = twist_ref[0]
+    cells, channels = grads[0].shape
+
+    @pl.when(pl.program_id(0) == 0)
+    def _():
+        for side in range(2):
+            for k in range(PARTS):
+                turned_grad_ref[side, k] = grads[side * PARTS + k][...].T
+        back_ref[...] = jnp.zeros_like(back_ref)
+
+    for side in range(2):
+        grad = jnp.zeros((cells, TILE), F32)
+        for k in range(PARTS):
+            grad = grad + jnp.dot(
+                grads[side * PARTS + k][...], wout_ref[twist ^ k], preferred_element_type=F32
+            )
+        grad_hidden_ref[side] = (grad * slope_ref[side]).astype(BF16)
+        for k in range(PARTS):
             back_ref[side, k] += lax.dot_general(
-                grad_hidden_ref[side], win_ref[twist ^ k], dims, preferred_element_type=F32
+                grad_hidden_ref[side], win_ref[twist ^ k], TURNED, preferred_element_type=F32
             )
     for j in range(PARTS):
         k = twist ^ j
@@ -445,52 +513,107 @@
 
     @pl.when(pl.program_id(0) == pl.num_programs(0) - 1)
     def _():
-        grad_own_ref[...] = back_ref[0].astype(BF16)
-        grad_far_ref[...] = back_ref[1].astype(BF16)
-        own_ref[...] = branch_ref[0].astype(BF16)
-        far_ref[...] = branch_ref[1].astype(BF16)
-
-
-def pointwise(twist, acts, win, wout, bias, units):
-    cells, channels = acts[0].shape
-    whole = lambda *shape: pl.BlockSpec(shape, lambda t: (0,) * len(shape), pipeline_mode=pl.Buffered(1))
-    tiled = lambda *shape: pl.BlockSpec(shape + (TILE,), lambda t: (0,) * len(shape) + (t,))
+        own_ref[...] = back_ref[0].astype(BF16)
+        far_ref[...] = back_ref[1].astype(BF16)
+
+
+def backward(twist, grads, turned, win, wout, active, slope, units):
+    cells, channels = grads[0].shape
     quad = jax.ShapeDtypeStruct((PARTS, cells, channels), BF16)
     return pl.pallas_call(
-        pointwise_kernel,
+        backward_kernel,
         grid=(win.shape[2] // TILE,),
-        out_shape=(quad,) * 4
-        + (
+        out_shape=(
+            quad,
+            quad,
             jax.ShapeDtypeStruct((2, channels + 8, units), F32),
             jax.ShapeDtypeStruct((2, channels + 8, units), BF16),
             jax.ShapeDtypeStruct((2, channels, units), F32),
             jax.ShapeDtypeStruct((2, channels, units), BF16),
         ),
         in_specs=[SMEM]
-        + [whole(cells, channels)] * (4 * PARTS)
-        + [tiled(PARTS, channels), tiled(PARTS, channels), tiled(1)],
-        out_specs=(whole(PARTS, cells, channels),) * 4
-        + (tiled(2, channels + 8), tiled(2, channels + 8), tiled(2, channels), tiled(2, channels)),
+        + [whole(cells, channels)] * (2 * PARTS)
+        + [
+            whole(2, PARTS, channels + 8, cells),
+            tiled(PARTS, channels),
+            tiled(PARTS, channels),
+            tiled(2, cells),
+            tiled(2, cells),
+        ],
+        out_specs=(
+            whole(PARTS, cells, channels),
+            whole(PARTS, cells, channels),
+            tiled(2, channels + 8),
+            tiled(2, channels + 8),
+            tiled(2, channels),
+            tiled(2, channels),
+        ),
         scratch_shapes=[
-            pltpu.VMEM((2, PARTS, channels + 8, cells), BF16),
             pltpu.VMEM((2, PARTS, channels, cells), BF16),
             pltpu.VMEM((2, PARTS, cells, channels), F32),
-            pltpu.VMEM((2, PARTS, cells, channels), F32),
-            pltpu.VMEM((2, cells, TILE), F32),
-            pltpu.VMEM((2, cells, TILE), F32),
-            pltpu.VMEM((2, cells, TILE), BF16),
             pltpu.VMEM((2, cells, TILE), BF16),
         ],
         compiler_params=pltpu.CompilerParams(vmem_limit_bytes=60 << 20, dimension_semantics=("arbitrary",)),
         cost_estimate=pl.CostEstimate(
-            flops=24 * cells * PARTS * channels * units, bytes_accessed=40 << 20, transcendentals=4 * cells * units
+            flops=16 * cells * PARTS * channels * units, bytes_accessed=50 << 20, transcendentals=0
         ),
-        name="pointwise",
-    )(twist, *acts, win, wout, bias)
-
-
-def picked(stack, index):
-    return lax.dynamic_index_in_dim(stack, index, 0, keepdims=False)
+        name="backward",
+    )(twist, *grads, turned, win, wout, active, slope)
+
+
+def join_kernel(own_ref, far_ref, *blocks):
+    for k in range(PARTS):
+        blocks[k][...] = (own_ref[k].astype(F32) + far_ref[k].astype(F32)).astype(BF16)
+
+
+def join(own, far):
+    block = jax.ShapeDtypeStruct(own.shape[1:], BF16)
+    return pl.pallas_call(
+        join_kernel,
+        out_shape=(block,) * PARTS,
+        in_specs=[VMEM, VMEM],
+        out_specs=(VMEM,) * PARTS,
+        compiler_params=pltpu.CompilerParams(vmem_limit_bytes=30 << 20),
+        cost_estimate=pl.CostEstimate(flops=own.size, bytes_accessed=6 * own.size, transcendentals=0),
+        name="join",
+    )(own, far)
+
+
+def gather_kernel(place_ref, *refs):
+    near, far = refs[:PARTS], refs[PARTS : 2 * PARTS]
+    in_ref, out_ref, bias_ref, held_ref = refs[2 * PARTS :]
+    core, quarter = place_ref[0], place_ref[1]
+    for shares, holder in ((near, core), (far, 1 - core)):
+        for step, share in enumerate(shares):
+            turn = (0, 1 << holder, 2 >> holder, 3)[step]
+            held_ref[holder, quarter ^ turn] = share[...]
+    channels = in_ref.shape[0] // PARTS
+    for c in range(PARTS):
+        in_ref[c * channels : (c + 1) * channels, :] = held_ref[0, c, 0:channels, :].astype(F32)
+        out_ref[:, c * channels : (c + 1) * channels] = held_ref[1, c, 0:channels, :].astype(F32).T
+    bias_ref[...] = held_ref[0, 0, channels : channels + 8, :].astype(F32)[0:1]
+
+
+def gather(place, near, far, channels):
+    rows, units = near[0].shape
+    return pl.pallas_call(
+        gather_kernel,
+        out_shape=(
+            jax.ShapeDtypeStruct((PARTS * channels, units), F32),
+            jax.ShapeDtypeStruct((units, PARTS * channels), F32),
+            jax.ShapeDtypeStruct((1, units), F32),
+        ),
+        in_specs=[SMEM] + [VMEM] * (2 * PARTS),
+        out_specs=(VMEM,) * 3,
+        scratch_shapes=[pltpu.VMEM((2, PARTS, rows, units), BF16)],
+        compiler_params=pltpu.CompilerParams(vmem_limit_bytes=40 << 20),
+        cost_estimate=pl.CostEstimate(flops=0, bytes_accessed=12 * PARTS * rows * units, transcendentals=0),
+        name="gather",
+    )(place, *near, *far)
+
+
+def after(value, *earlier):
+    return lax.optimization_barrier((value, earlier))[0]
 
 
 def body(
@@ -524,18 +647,19 @@
             lax.dynamic_slice_in_dim(weight_out, quarter * part, part, 1).T,
         ]
     )
+    rest = bias_in.reshape(1, units)
+    digits = []
+    for _ in range(3):
+        digits.append(lax.reduce_precision(rest, 8, 7))
+        rest = rest - digits[-1]
+    piece = jnp.concatenate(
+        [piece.reshape(2 * part, units)] + [digit.astype(BF16) for digit in digits] + [jnp.zeros((5, units), BF16)]
+    )
     owner = lambda at, lev: lev // 2 == core_of(at)
-    near = [
-        tuple(
-            routed(value, owner, lambda at, lev, k=k: (at, lev ^ k)) for value in (piece, bias_in.reshape(1, units))
-        )
-        for k in (1, 2, 3)
-    ]
-    first = [jnp.where(mine, own, far) for own, far in zip((piece, bias_in.reshape(1, units)), near[1])]
-    second = [jnp.where(mine, one, far) for one, far in zip(near[0], near[2])]
-    slab = jnp.concatenate([first[0], second[0]], axis=2)
-    win_rows = [slab[0]]
-    wout_rows = [slab[1]]
+    near = [routed(piece, owner, lambda at, lev, k=k: (at, lev ^ k)) for k in (1, 2, 3)]
+    slab = jnp.concatenate([jnp.where(mine, piece, near[1]), jnp.where(mine, near[0], near[2])], axis=1)
+    win_rows = [slab[:part]]
+    wout_rows = [slab[part : 2 * part]]
     win_rows += [flipped(win_rows[0], "dp", 2)]
     win_rows += [flipped(value, "dp", 4) for value in win_rows]
     across_wout = flipped(wout_rows[0], "dp", 4)
@@ -543,7 +667,8 @@
     room = -2 * units % TILE
     widen = lambda rows: jnp.pad(jnp.stack(rows), ((0, 0), (0, 0), (0, room)))
     win, wout = widen(win_rows), widen(wout_rows)
-    bias_hidden = jnp.pad(jnp.concatenate([first[1], second[1]], axis=1), ((0, 0), (0, room)))
+    digits = slab[2 * part : 2 * part + 3].astype(F32)
+    bias_hidden = jnp.pad(digits[0:1] + digits[1:2] + digits[2:3], ((0, 0), (0, room)))
 
     sample = place // SPAN
     count_here = jnp.sum(jnp.where(jnp.arange(counts.shape[0]) == sample, counts, 0))
@@ -558,22 +683,24 @@
     taps = by_lane_tile(kernel.reshape(49, channels))
     row = lambda vector: vector.reshape(1, channels)
     conv, stat = depthwise(scalar(core), inputs, rim, wet, keep, taps, by_lane_tile(row(conv_bias))[:, 0])
-    *grad_blocks, grad_bias_out = cut(scalar(level), cotangent, wet)
     *normed_blocks, fit = norm(scalar(level), conv, stat, flipped(stat, "dp", 1), row(norm_gain), row(norm_bias))
+    *grad_blocks, grad_bias_out = cut(scalar(level), after(cotangent, normed_blocks), wet)
 
     spread_out = lambda blocks: [blocks[0]] + [flipped(blocks[k], "chan", k) for k in range(1, PARTS)]
-    grad_cells = spread_out(grad_blocks)
+    other_core = lambda blocks: [flipped(block, "dp", 1) for block in blocks]
+    twist = scalar(level ^ quarter)
     normed_cells = spread_out(normed_blocks)
-    other_core = lambda blocks: [flipped(block, "dp", 1) for block in blocks]
-    acts = normed_cells + other_core(normed_cells) + grad_cells + other_core(grad_cells)
-    back_own, back_far, branch_own, branch_far, in_keep, in_send, out_keep, out_send = pointwise(
-        scalar(level ^ quarter), acts, win, wout, bias_hidden, 2 * units
-    )
-    joined = lambda own, far: [
-        (own[k].astype(F32) + far[k].astype(F32)).astype(BF16) for k in range(PARTS)
-    ]
-    back_blocks = spread_out(joined(back_own, flipped(back_far, "dp", 1)))
-    branch_blocks = spread_out(joined(branch_own, flipped(branch_far, "dp", 1)))
+    grad_cells = spread_out(after(grad_blocks, normed_cells))
+    branch_own, branch_far, active, slope, turned = forward(
+        twist, normed_cells + other_core(normed_cells), win, wout, bias_hidden
+    )
+    branch_blocks = join(branch_own, flipped(branch_far, "dp", 1))
+    back_own, back_far, in_keep, in_send, out_keep, out_send = backward(
+        twist, grad_cells + other_core(grad_cells), turned, win, wout, active, slope, 2 * units
+    )
+    joined = join(back_own, flipped(back_far, "dp", 1))
+    branch_blocks = spread_out(after(branch_blocks, grad_cells))
+    back_blocks = spread_out(joined)
 
     sums = moments(scalar(level), conv, fit, back_blocks)
     grad_conv, outgoing_grad, grad_conv_bias = norm_back(
@@ -581,7 +708,6 @@
     )
     grad_rim = flipped(outgoing_grad, "dp", 1)
     grad_inputs, grad_taps = depthwise_back(scalar(core), grad_conv, grad_rim, inputs, cotangent, wet, keep, taps)
-    output = finish(scalar(level), inputs, wet, keep, row(bias_out), branch_blocks)
     small = jnp.concatenate([grad_taps, grad_conv_bias, sums[1:2], sums[0:1], grad_bias_out, jnp.zeros((3, channels), F32)])
     bit = 1
     while bit < lax.axis_size("dp"):
@@ -589,40 +715,36 @@
         bit *= 2
 
     wide = lambda value: value.astype(F32)
+    in_send, out_send = after((in_send, out_send), joined)
     in_two = in_keep + wide(flipped(in_send, "dp", 2))
     out_two = out_keep + wide(flipped(out_send, "dp", 4))
     in_one = in_two[0] + wide(flipped(in_two[1].astype(BF16), "dp", 4))
     out_one = out_two[0] + wide(flipped(out_two[1].astype(BF16), "dp", 2))
     both = jnp.concatenate([in_one, out_one])
-    low = both.astype(BF16)
+    low = after(both.astype(BF16), back_blocks)
     stranger = lambda at, lev: not owner(at, lev)
-    total = (
-        both[:, :units]
-        + wide(routed(low[:, units:], owner, lambda at, lev: (at, lev ^ 1)))
-        + wide(routed(low[:, :units], stranger, lambda at, lev: (at, lev ^ 2)))
-        + wide(routed(low[:, units:], stranger, lambda at, lev: (at, lev ^ 3)))
-    )
+    arrived = (
+        routed(low[:, units:], owner, lambda at, lev: (at, lev ^ 1)),
+        routed(low[:, :units], stranger, lambda at, lev: (at, lev ^ 2)),
+        routed(low[:, units:], stranger, lambda at, lev: (at, lev ^ 3)),
+    )
+    output = finish(scalar(level), inputs, wet, keep, row(bias_out), branch_blocks)
+    arrived = after(arrived, grad_taps)
+    total = both[:, :units] + wide(arrived[0]) + wide(arrived[1]) + wide(arrived[2])
     bit = SPAN * PARTS
     while bit < lax.axis_size("dp"):
         total = total + flipped(total, "dp", bit)
         bit *= 2
     held = total.astype(BF16)
     held = jnp.where(mine, held, flipped(held, "dp", 1))
-    share = jnp.where(core == 0, held[: channels + 8], jnp.pad(held[channels + 8 :], ((0, 8), (0, 0))))
+    share = jnp.where(core == 0, held[: part + 8], jnp.pad(held[part + 8 :], ((0, 8), (0, 0))))
     always = lambda at, lev: True
     turn = lambda value, step: routed(value, always, lambda at, lev: (at ^ (2 << (core_of(at) ^ step)), lev))
     one = turn(share, 0)
-    two = turn(share, 1)
-    three = turn(one, 1)
-    shares = jnp.stack([share, jnp.where(core == 0, one, two), jnp.where(core == 0, two, one), three])
-    others = flipped(shares, "dp", 1)
-    in_shares = jnp.where(core == 0, shares, others)
-    out_shares = jnp.where(core == 0, others, shares)
-    ordered_in = [picked(in_shares, quarter ^ c) for c in range(PARTS)]
-    ordered_out = [picked(out_shares, quarter ^ c)[:channels] for c in range(PARTS)]
-    grad_weight_in = jnp.concatenate([value[:channels] for value in ordered_in]).astype(F32)
-    grad_weight_out = jnp.concatenate(ordered_out).astype(F32).T
-    grad_bias_in = ordered_in[0][channels].astype(F32)
+    shares = [share, one, turn(share, 1), turn(one, 1)]
+    grad_weight_in, grad_weight_out, grad_bias_in = gather(
+        jnp.stack([core, quarter]).astype(jnp.int32), shares, other_core(shares), part
+    )
     return (
         output,
         grad_inputs,
@@ -631,7 +753,7 @@
         small[50],
         small[51],
         grad_weight_in,
-        grad_bias_in,
+        grad_bias_in.reshape(units),
         grad_weight_out,
         small[52],
     )

time: 490 us -> 461 us (0.941); the launches traced: 489 us -> 453 us
  Pallas kernels: 122 us -> 145 us
  starting transfers between devices: 102 us -> 82.6 us
  waiting for transfers between devices: 186 us -> 172 us
  other arithmetic: 31.8 us -> 18.2 us
  local copies, waits for them, and re-layouts: 45.3 us -> 33.5 us
    ppermute x12 -> x9, waiting for transfers between devices: 58.9 us -> 20.8 us  [routed(): return lax.ppermute(block, ('dp', 'chan'), route)]
    ppermute x41 -> x44, waiting for transfers between devices: 127 us -> 152 us  [flipped(): lax.ppermute(block, axis, [(place, place ^ bit) for place in range(count)])]
    pallas_call x1 -> x5, Pallas kernels: 56 us -> 80 us  [the longest x1 41.9 us: backward(): pl.pallas_call(backward_kernel, grid=(win.shape[2] // TILE,), out_shape=(...]
    ppermute x12 -> x9, starting transfers between devices: 47.9 us -> 26.1 us  [routed(): return lax.ppermute(block, ('dp', 'chan'), route)]
    unnamed x110 -> x76, local copies, waits for them, and re-layouts: 30 us -> 15 us
    convert_element_type x5 -> x2, other arithmetic: 7.44 us -> 0.17 us  [the longest x1 0.16 us: body(): low = after(both.astype(BF16), back_blocks)]
    ppermute x0 -> x2, local copies, waits for them, and re-layouts: none -> 6.4 us  [flipped(): lax.ppermute(block, axis, [(place, place ^ bit) for place in range(count)])]
    slice x4 -> x1, local copies, waits for them, and re-layouts: 5.38 us -> 0.03 us  [body(): held[part + 8:]]
  transfers between devices with their start and end apart: 53 -> 53, of which waited for: 21 -> 20; matrix products, arithmetic and copies ran while one was open for 9% -> 5% of each run, Pallas kernels for 13% -> 21%
where the time goes in v2:
time: 461 us; the launch traced here: 453 us
  waiting for transfers between devices  172 us (37%)
  Pallas kernels  145 us (31%)
  starting transfers between devices  82.6 us (18%)
  local copies, waits for them, and re-layouts  33.5 us (7%)
  other arithmetic  18.2 us (4%)
    ppermute x44, waiting for transfers between devices, flipped(): lax.ppermute(block, axis, [(place, place ^ bit) for place in range(count)])  152 us
    ppermute x44, starting transfers between devices, flipped(): lax.ppermute(block, axis, [(place, place ^ bit) for place in range(count)])  56.4 us
    pallas_call x1, Pallas kernels, backward(): pl.pallas_call(backward_kernel, grid=(win.shape[2] // TILE,), out_shape=(...  41.9 us
    pallas_call x1, Pallas kernels, forward(): pl.pallas_call(forward_kernel, grid=(units // TILE,), out_shape=(quad, qu...  31.8 us
    pallas_call x1, Pallas kernels, depthwise_back(): pl.pallas_call(depthwise_back_kernel, out_shape=(jax.ShapeDtypeStruct(x.s...  31.5 us
    ppermute x9, starting transfers between devices, routed(): return lax.ppermute(block, ('dp', 'chan'), route)  26.1 us
    pallas_call x1, Pallas kernels, depthwise(): pl.pallas_call(depthwise_kernel, out_shape=(jax.ShapeDtypeStruct(x.shape,...  23 us
    ppermute x9, waiting for transfers between devices, routed(): return lax.ppermute(block, ('dp', 'chan'), route)  20.8 us
  transfers between devices with their start and end apart: 53, of which 20 were waited for; matrix products, arithmetic and copies ran while one was open for 5% of the time, Pallas kernels for 21%

profile of v2, /device:TPU:0, one launch (start us, length us, event | category | flops | bytes accessed | tf_op | source)
XLA Modules:
  0.0 453.3 jit_solution(5988241369260521598)
XLA Ops:
  4.8 6.0 %collective-permute-start.9 = (bf16[408,800]{1,0:T(8,128)(2,1)S(1)}, bf16[408,800]{1,0:T(8,128)(2,1)S(1)}, u32[]{:S(2)}, u32[]{:S(2)}) collective-permute-start(bf16[408,800]{1,0:T(8,128)(2,1)S(1)} %concatenate.12), channel_id=1, source_target_pairs={{0,2},{1,3},{6,4},{7,5},{8,10},{9,11},{14,12},{15,13},{16,18},{17,... | collective-permute-start | bytes 1958408 | tf_op jit(solution)/shard_map/ppermute | solution.py:36
  19.8 18.2 %collective-permute-done.10 = bf16[408,800]{1,0:T(8,128)(2,1)S(1)} collective-permute-done((bf16[408,800]{1,0:T(8,128)(2,1)S(1)}, bf16[408,800]{1,0:T(8,128)(2,1)S(1)}, u32[]{:S(2)}, u32[]{:S(2)}) %collective-permute-start.10) | collective-permute-done | bytes 652832 | tf_op jit(solution)/shard_map/ppermute | solution.py:36
  45.9 23.0 %depthwise.1 = (f32[24,152,200]{2,1,0:T(8,128)S(1)}, f32[2,200]{1,0:T(2,128)S(1)}) custom-call(s32[1]{0:T(128)} %bitcast.4.within_ref, bf16[24,152,200]{2,1,0:T(8,128)(2,1)S(1)} %copy-done.6, bf16[3,152,200]{2,1,0:T(8,128)(2,1)S(1)} %collective-permute-done.rim_ref, f32[24,152,1]{2,1,0:T(8,128)S(1)} %copy.38.wet_ref, ...), custom_call_target="tpu_custom_call" | custom-call | flops 71500800 | bytes 4377600 | tf_op jit(solution)/shard_map/depthwise/pallas_call | solution.py:118
  74.0 6.0 %collective-permute-start.2 = (bf16[912,200]{1,0:T(8,128)(2,1)S(1)}, bf16[912,200]{1,0:T(8,128)(2,1)S(1)}, u32[]{:S(2)}, u32[]{:S(2)}) collective-permute-start(bf16[912,200]{1,0:T(8,128)(2,1)S(1)} %get-tuple-element.67), channel_id=1, source_target_pairs={{0,1},{1,0},{2,3},{3,2},{4,5},{5,4},{6,7},{7,6},{8,9},{9,8},{10,11... | collective-permute-start | bytes 1094408 | tf_op jit(solution)/shard_map/ppermute | solution.py:25
  85.5 13.6 %collective-permute-done.2.refs_1_ = bf16[912,200]{1,0:T(8,128)(2,1)S(1)} collective-permute-done((bf16[912,200]{1,0:T(8,128)(2,1)S(1)}, bf16[912,200]{1,0:T(8,128)(2,1)S(1)}, u32[]{:S(2)}, u32[]{:S(2)}) %collective-permute-start.2) | collective-permute-done | bytes 364832 | tf_op jit(solution)/shard_map/ppermute | solution.py:25
  104.2 14.1 %collective-permute-done.3.refs_2_ = bf16[912,200]{1,0:T(8,128)(2,1)} collective-permute-done((bf16[912,200]{1,0:T(8,128)(2,1)}, bf16[912,200]{1,0:T(8,128)(2,1)}, u32[]{:S(2)}, u32[]{:S(2)}) %collective-permute-start.3) | collective-permute-done | bytes 364832 | tf_op jit(solution)/shard_map/ppermute | solution.py:25
  118.4 8.8 %collective-permute-start.19 = (bf16[912,200]{1,0:T(8,128)(2,1)S(1)}, bf16[912,200]{1,0:T(8,128)(2,1)S(1)}, u32[]{:S(2)}, u32[]{:S(2)}) collective-permute-start(bf16[912,200]{1,0:T(8,128)(2,1)S(1)} %get-tuple-element.82), channel_id=1, source_target_pairs={{0,1},{1,0},{2,3},{3,2},{4,5},{5,4},{6,7},{7,6},{8,9},{9,8},{10,11... | collective-permute-start | bytes 1094408 | tf_op jit(solution)/shard_map/ppermute | solution.py:25
  130.9 3.8 fusion.10.refs_8_.refs_9_
  138.2 8.6 %collective-permute-done.15 = bf16[200,1600]{1,0:T(8,128)(2,1)S(1)} collective-permute-done((bf16[200,1600]{1,0:T(8,128)(2,1)}, bf16[200,1600]{1,0:T(8,128)(2,1)S(1)}, u32[]{:S(2)}, u32[]{:S(2)}) %collective-permute-start.15) | collective-permute-done | bytes 640032 | tf_op jit(solution)/shard_map/ppermute | solution.py:25
  146.8 13.8 %collective-permute-done.17 = bf16[200,1600]{1,0:T(8,128)(2,1)S(1)} collective-permute-done((bf16[200,1600]{1,0:T(8,128)(2,1)}, bf16[200,1600]{1,0:T(8,128)(2,1)S(1)}, u32[]{:S(2)}, u32[]{:S(2)}) %collective-permute-start.17) | collective-permute-done | bytes 640032 | tf_op jit(solution)/shard_map/ppermute | solution.py:25
  164.9 4.2 collective-permute-done.20.refs_2_
  169.7 31.8 %forward.1 = (bf16[4,912,200]{2,1,0:T(8,128)(2,1)}, bf16[4,912,200]{2,1,0:T(8,128)(2,1)}, bf16[2,912,1792]{2,1,0:T(8,128)(2,1)}, f32[2,912,1792]{2,1,0:T(8,128)}, bf16[2,4,208,912]{3,2,1,0:T(8,128)(2,1)}) custom-call(s32[1]{0:T(128)} %bitcast.3.twist_ref, bf16[912,200]{1,0:T(8,128)(2,1)} %copy-done.17, bf16[912,200]{1,0:T(8,128)(2,1)} %copy-done.27, ...), custom_call_target="tpu_custom_call" | custom-call | flops 10459545600 | bytes 33554432 | tf_op jit(solution)/shard_map/forward/pallas_call | solution.py:439
  202.5 41.9 %backward.1 = (bf16[4,912,200]{2,1,0:T(8,128)(2,1)}, bf16[4,912,200]{2,1,0:T(8,128)(2,1)}, f32[2,208,1600]{2,1,0:T(8,128)}, bf16[2,208,1600]{2,1,0:T(8,128)(2,1)...) custom-call(s32[1]{0:T(128)} %bitcast.3.twist_ref, bf16[912,200]{1,0:T(8,128)(2,1)} %copy-done.18, ...), custom_call_target="tpu_custom_call" | custom-call | flops 18677760000 | bytes 52428800 | tf_op jit(solution)/shard_map/backward/pallas_call | solution.py:523
  256.7 30.4 %collective-permute-done.40 = bf16[2,200,1600]{2,1,0:T(8,128)(2,1)S(1)} collective-permute-done((bf16[2,200,1600]{2,1,0:T(8,128)(2,1)}, bf16[2,200,1600]{2,1,0:T(8,128)(2,1)S(1)}, u32[]{:S(2)}, u32[]{:S(2)}) %collective-permute-start.40) | collective-permute-done | bytes 1280032 | tf_op jit(solution)/shard_map/ppermute | solution.py:25
  290.6 9.4 %collective-permute-start.30 = (bf16[912,200]{1,0:T(8,128)(2,1)S(1)}, bf16[912,200]{1,0:T(8,128)(2,1)S(1)}, u32[]{:S(2)}, u32[]{:S(2)}) collective-permute-start(bf16[912,200]{1,0:T(8,128)(2,1)S(1)} %get-tuple-element.96), channel_id=1, source_target_pairs={{0,1},{1,0},{2,3},{3,2},{4,5},{5,4},{6,7},{7,6},{8,9},{9,8},{10,11... | collective-permute-start | bytes 1094408 | tf_op jit(solution)/shard_map/ppermute | solution.py:25
  306.5 12.2 %collective-permute-done.30.refs_1_ = bf16[912,200]{1,0:T(8,128)(2,1)S(1)} collective-permute-done((bf16[912,200]{1,0:T(8,128)(2,1)S(1)}, bf16[912,200]{1,0:T(8,128)(2,1)S(1)}, u32[]{:S(2)}, u32[]{:S(2)}) %collective-permute-start.30) | collective-permute-done | bytes 364832 | tf_op jit(solution)/shard_map/ppermute | solution.py:25
  318.7 15.8 %collective-permute-done.31.refs_2_ = bf16[912,200]{1,0:T(8,128)(2,1)S(1)} collective-permute-done((bf16[912,200]{1,0:T(8,128)(2,1)S(1)}, bf16[912,200]{1,0:T(8,128)(2,1)S(1)}, u32[]{:S(2)}, u32[]{:S(2)}) %collective-permute-start.31) | collective-permute-done | bytes 364832 | tf_op jit(solution)/shard_map/ppermute | solution.py:25
  334.8 10.1 %collective-permute-start.42 = (bf16[408,800]{1,0:T(8,128)(2,1)S(1)}, bf16[408,800]{1,0:T(8,128)(2,1)S(1)}, u32[]{:S(2)}, u32[]{:S(2)}) collective-permute-start(bf16[408,800]{1,0:T(8,128)(2,1)S(1)} %get-tuple-element.121), channel_id=1, source_target_pairs={{0,1},{1,0},{6,7},{7,6},{8,9},{9,8},{14,15},{15,14},{16,17},{17,16... | collective-permute-start | bytes 1958408 | tf_op jit(solution)/shard_map/ppermute | solution.py:36
  355.4 31.5 %depthwise_back.1 = (f32[24,152,200]{2,1,0:T(8,128)}, f32[49,200]{1,0:T(8,128)S(1)}) custom-call(s32[1]{0:T(128)} %bitcast.4.within_ref, f32[24,152,200]{2,1,0:T(8,128)} %copy-done.11, bf16[3,152,200]{2,1,0:T(8,128)(2,1)S(1)} %collective-permute-done.34.rim_ref, bf16[24,152,200]{2,1,0:T(8,128)(2,1)S(1)} %copy-done.7, bf16[24,152,200]{2,1,0:T(8,128)(2,1)S(1)} %copy-done.10, ...), custom_call_target="tpu_custom_call" | custom-call | flops 143001600 | bytes 8755200 | tf_op jit(solution)/shard_map/depthwise_back/pallas_call | solution.py:181
  397.9 3.7 copy.36.far_ref
  405.8 4.1 collective-permute-start.23
  411.9 15.2 %collective-permute-done.22.refs_1_ = bf16[912,200]{1,0:T(8,128)(2,1)S(1)} collective-permute-done((bf16[912,200]{1,0:T(8,128)(2,1)S(1)}, bf16[912,200]{1,0:T(8,128)(2,1)S(1)}, u32[]{:S(2)}, u32[]{:S(2)}) %collective-permute-start.22) | collective-permute-done | bytes 364832 | tf_op jit(solution)/shard_map/ppermute | solution.py:25
  428.7 12.7 %collective-permute-done.23.refs_2_ = bf16[912,200]{1,0:T(8,128)(2,1)S(1)} collective-permute-done((bf16[912,200]{1,0:T(8,128)(2,1)S(1)}, bf16[912,200]{1,0:T(8,128)(2,1)S(1)}, u32[]{:S(2)}, u32[]{:S(2)}) %collective-permute-start.23) | collective-permute-done | bytes 364832 | tf_op jit(solution)/shard_map/ppermute | solution.py:25
  447.3 5.5 %gather.1 = (f32[800,800]{1,0:T(8,128)}, f32[800,800]{1,0:T(8,128)}, f32[1,800]{1,0:T(1,128)S(1)}) custom-call(s32[2]{0:T(128)S(1)} %pad_add_fusion.place_ref, bf16[208,800]{1,0:T(8,128)(2,1)} %slice_select_fusion.refs_0_, bf16[208,800]{1,0:T(8,128)(2,1)} %collective-permute-done.46.refs_1_, bf16[208,800]{1,0:T(8,128)(2,1)} %collective-permute-done.47.refs_2_, ...), custom_call_target="tpu_custom_call" | custom-call | bytes 7987200 | tf_op jit(solution)/shard_map/gather/pallas_call | solution.py:599
  (226 shorter events, 107.6 us)
Async XLA Ops:
  39.5 42.5 %collective-permute-start.12 = (bf16[200,1600]{1,0:T(8,128)(2,1)}, bf16[200,1600]{1,0:T(8,128)(2,1)}, u32[]{:S(2)}, u32[]{:S(2)}) collective-permute-start(bf16[200,1600]{1,0:T(8,128)(2,1)} %get-tuple-element.119), channel_id=1, source_target_pairs={{0,8},{4,12},{8,0},{12,4},{16,24},{20,28},{24,16},{28,20},{1,9},{5... | collective-permute-start | bytes 1920008 | tf_op jit(solution)/shard_map/ppermute | solution.py:25
  80.0 48.8 %collective-permute-start.13 = (bf16[200,1600]{1,0:T(8,128)(2,1)}, bf16[200,1600]{1,0:T(8,128)(2,1)}, u32[]{:S(2)}, u32[]{:S(2)}) collective-permute-start(bf16[200,1600]{1,0:T(8,128)(2,1)} %get-tuple-element.119), channel_id=1, source_target_pairs={{0,16},{4,20},{8,24},{12,28},{16,0},{20,4},{24,8},{28,12},{1,17},{... | collective-permute-start | bytes 1920008 | tf_op jit(solution)/shard_map/ppermute | solution.py:25
  81.5 47.3 %collective-permute-start.16 = (bf16[200,1600]{1,0:T(8,128)(2,1)}, bf16[200,1600]{1,0:T(8,128)(2,1)}, u32[]{:S(2)}, u32[]{:S(2)}) collective-permute-start(bf16[200,1600]{1,0:T(8,128)(2,1)} %get-tuple-element.118), channel_id=1, source_target_pairs={{0,16},{4,20},{8,24},{12,28},{16,0},{20,4},{24,8},{28,12},{1,17},{... | collective-permute-start | bytes 1920008 | tf_op jit(solution)/shard_map/ppermute | solution.py:25
  82.0 47.4 %collective-permute-start.14 = (bf16[200,1600]{1,0:T(8,128)(2,1)}, bf16[200,1600]{1,0:T(8,128)(2,1)}, u32[]{:S(2)}, u32[]{:S(2)}) collective-permute-start(bf16[200,1600]{1,0:T(8,128)(2,1)} %collective-permute-done.12), channel_id=1, source_target_pairs={{0,16},{4,20},{8,24},{12,28},{16,0},{20,4},{24,8},{28,12},{1,17},{... | collective-permute-start | bytes 1920008 | tf_op jit(solution)/shard_map/ppermute | solution.py:25
  83.5 34.9 %collective-permute-start.3 = (bf16[912,200]{1,0:T(8,128)(2,1)}, bf16[912,200]{1,0:T(8,128)(2,1)}, u32[]{:S(2)}, u32[]{:S(2)}) collective-permute-start(bf16[912,200]{1,0:T(8,128)(2,1)} %get-tuple-element.68), channel_id=1, source_target_pairs={{0,2},{1,3},{2,0},{3,1},{4,6},{5,7},{6,4},{7,5},{8,10},{9,11},{10,... | collective-permute-start | bytes 1094408 | tf_op jit(solution)/shard_map/ppermute | solution.py:25
  118.4 46.4 %collective-permute-start.19 = (bf16[912,200]{1,0:T(8,128)(2,1)S(1)}, bf16[912,200]{1,0:T(8,128)(2,1)S(1)}, u32[]{:S(2)}, u32[]{:S(2)}) collective-permute-start(bf16[912,200]{1,0:T(8,128)(2,1)S(1)} %get-tuple-element.82), channel_id=1, source_target_pairs={{0,1},{1,0},{2,3},{3,2},{4,5},{5,4},{6,7},{7,6},{8,9},{9,8},{10,11... | collective-permute-start | bytes 1094408 | tf_op jit(solution)/shard_map/ppermute | solution.py:25
  129.4 31.2 %collective-permute-start.17 = (bf16[200,1600]{1,0:T(8,128)(2,1)}, bf16[200,1600]{1,0:T(8,128)(2,1)S(1)}, u32[]{:S(2)}, u32[]{:S(2)}) collective-permute-start(bf16[200,1600]{1,0:T(8,128)(2,1)} %collective-permute-done.16), channel_id=1, source_target_pairs={{0,8},{4,12},{8,0},{12,4},{16,24},{20,28},{24,16},{28,20},{1,9},{5... | collective-permute-start | bytes 1920008 | tf_op jit(solution)/shard_map/ppermute | solution.py:25
  134.7 34.4 %collective-permute-start.20 = (bf16[912,200]{1,0:T(8,128)(2,1)S(1)}, bf16[912,200]{1,0:T(8,128)(2,1)S(1)}, u32[]{:S(2)}, u32[]{:S(2)}) collective-permute-start(bf16[912,200]{1,0:T(8,128)(2,1)S(1)} %get-tuple-element.83), channel_id=1, source_target_pairs={{0,2},{1,3},{2,0},{3,1},{4,6},{5,7},{6,4},{7,5},{8,10},{9,11},{10,... | collective-permute-start | bytes 1094408 | tf_op jit(solution)/shard_map/ppermute | solution.py:25
  136.6 32.4 %collective-permute-start.21 = (bf16[912,200]{1,0:T(8,128)(2,1)S(1)}, bf16[912,200]{1,0:T(8,128)(2,1)S(1)}, u32[]{:S(2)}, u32[]{:S(2)}) collective-permute-start(bf16[912,200]{1,0:T(8,128)(2,1)S(1)} %get-tuple-element.84), channel_id=1, source_target_pairs={{0,3},{1,2},{2,1},{3,0},{4,7},{5,6},{6,5},{7,4},{8,11},{9,10},{10,... | collective-permute-start | bytes 1094408 | tf_op jit(solution)/shard_map/ppermute | solution.py:25
  164.2 37.3 %collective-permute-start.25 = (bf16[912,200]{1,0:T(8,128)(2,1)S(1)}, bf16[912,200]{1,0:T(8,128)(2,1)S(1)}, u32[]{:S(2)}, u32[]{:S(2)}) collective-permute-start(bf16[912,200]{1,0:T(8,128)(2,1)S(1)} %get-tuple-element.81.refs_0_), channel_id=1, source_target_pairs={{0,4},{4,0},{8,12},{12,8},{16,20},{20,16},{24,28},{28,24},{1,5},{5... | collective-permute-start | bytes 1094408 | tf_op jit(solution)/shard_map/ppermute | solution.py:25
  164.8 36.7 %collective-permute-start.26 = (bf16[912,200]{1,0:T(8,128)(2,1)S(1)}, bf16[912,200]{1,0:T(8,128)(2,1)S(1)}, u32[]{:S(2)}, u32[]{:S(2)}) collective-permute-start(bf16[912,200]{1,0:T(8,128)(2,1)S(1)} %collective-permute-done.19.refs_1_), channel_id=1, source_target_pairs={{0,4},{4,0},{8,12},{12,8},{16,20},{20,16},{24,28},{28,24},{1,5},{5... | collective-permute-start | bytes 1094408 | tf_op jit(solution)/shard_map/ppermute | solution.py:25
  169.1 32.5 %collective-permute-start.27 = (bf16[912,200]{1,0:T(8,128)(2,1)S(1)}, bf16[912,200]{1,0:T(8,128)(2,1)}, u32[]{:S(2)}, u32[]{:S(2)}) collective-permute-start(bf16[912,200]{1,0:T(8,128)(2,1)S(1)} %collective-permute-done.20.refs_2_), channel_id=1, source_target_pairs={{0,4},{4,0},{8,12},{12,8},{16,20},{20,16},{24,28},{28,24},{1,5},{5... | collective-permute-start | bytes 1094408 | tf_op jit(solution)/shard_map/ppermute | solution.py:25
  169.1 32.5 %collective-permute-start.28 = (bf16[912,200]{1,0:T(8,128)(2,1)S(1)}, bf16[912,200]{1,0:T(8,128)(2,1)}, u32[]{:S(2)}, u32[]{:S(2)}) collective-permute-start(bf16[912,200]{1,0:T(8,128)(2,1)S(1)} %collective-permute-done.21.refs_3_), channel_id=1, source_target_pairs={{0,4},{4,0},{8,12},{12,8},{16,20},{20,16},{24,28},{28,24},{1,5},{5... | collective-permute-start | bytes 1094408 | tf_op jit(solution)/shard_map/ppermute | solution.py:25
  255.7 31.5 %collective-permute-start.40 = (bf16[2,200,1600]{2,1,0:T(8,128)(2,1)}, bf16[2,200,1600]{2,1,0:T(8,128)(2,1)S(1)}, u32[]{:S(2)}, u32[]{:S(2)}) collective-permute-start(bf16[2,200,1600]{2,1,0:T(8,128)(2,1)} %get-tuple-element.110), channel_id=1, source_target_pairs={{0,16},{4,20},{8,24},{12,28},{16,0},{20,4},{24,8},{28,12},{1,17},{... | collective-permute-start | bytes 3840008 | tf_op jit(solution)/shard_map/ppermute | solution.py:25
  256.2 32.3 %collective-permute-start.38 = (bf16[2,208,1600]{2,1,0:T(8,128)(2,1)}, bf16[2,208,1600]{2,1,0:T(8,128)(2,1)S(1)}, u32[]{:S(2)}, u32[]{:S(2)}) collective-permute-start(bf16[2,208,1600]{2,1,0:T(8,128)(2,1)} %get-tuple-element.108), channel_id=1, source_target_pairs={{0,8},{4,12},{8,0},{12,4},{16,24},{20,28},{24,16},{28,20},{1,9},{5... | collective-permute-start | bytes 3993608 | tf_op jit(solution)/shard_map/ppermute | solution.py:25
  299.9 34.5 %collective-permute-start.31 = (bf16[912,200]{1,0:T(8,128)(2,1)S(1)}, bf16[912,200]{1,0:T(8,128)(2,1)S(1)}, u32[]{:S(2)}, u32[]{:S(2)}) collective-permute-start(bf16[912,200]{1,0:T(8,128)(2,1)S(1)} %get-tuple-element.97), channel_id=1, source_target_pairs={{0,2},{1,3},{2,0},{3,1},{4,6},{5,7},{6,4},{7,5},{8,10},{9,11},{10,... | collective-permute-start | bytes 1094408 | tf_op jit(solution)/shard_map/ppermute | solution.py:25
  301.3 33.2 %collective-permute-start.32 = (bf16[912,200]{1,0:T(8,128)(2,1)S(1)}, bf16[912,200]{1,0:T(8,128)(2,1)S(1)}, u32[]{:S(2)}, u32[]{:S(2)}) collective-permute-start(bf16[912,200]{1,0:T(8,128)(2,1)S(1)} %get-tuple-element.98), channel_id=1, source_target_pairs={{0,3},{1,2},{2,1},{3,0},{4,7},{5,6},{6,5},{7,4},{8,11},{9,10},{10,... | collective-permute-start | bytes 1094408 | tf_op jit(solution)/shard_map/ppermute | solution.py:25
  334.8 52.1 %collective-permute-start.42 = (bf16[408,800]{1,0:T(8,128)(2,1)S(1)}, bf16[408,800]{1,0:T(8,128)(2,1)S(1)}, u32[]{:S(2)}, u32[]{:S(2)}) collective-permute-start(bf16[408,800]{1,0:T(8,128)(2,1)S(1)} %get-tuple-element.121), channel_id=1, source_target_pairs={{0,1},{1,0},{6,7},{7,6},{8,9},{9,8},{14,15},{15,14},{16,17},{17,16... | collective-permute-start | bytes 1958408 | tf_op jit(solution)/shard_map/ppermute | solution.py:36
  345.0 42.0 %collective-permute-start.43 = (bf16[408,800]{1,0:T(8,128)(2,1)S(1)}, bf16[408,800]{1,0:T(8,128)(2,1)S(1)}, u32[]{:S(2)}, u32[]{:S(2)}) collective-permute-start(bf16[408,800]{1,0:T(8,128)(2,1)S(1)} %get-tuple-element.120), channel_id=1, source_target_pairs={{2,0},{3,1},{4,6},{5,7},{10,8},{11,9},{12,14},{13,15},{18,16},{19,... | collective-permute-start | bytes 1958408 | tf_op jit(solution)/shard_map/ppermute | solution.py:36
  346.3 40.7 %collective-permute-start.44 = (bf16[408,800]{1,0:T(8,128)(2,1)S(1)}, bf16[408,800]{1,0:T(8,128)(2,1)S(1)}, u32[]{:S(2)}, u32[]{:S(2)}) collective-permute-start(bf16[408,800]{1,0:T(8,128)(2,1)S(1)} %get-tuple-element.121), channel_id=1, source_target_pairs={{2,1},{3,0},{4,7},{5,6},{10,9},{11,8},{12,15},{13,14},{18,17},{19,... | collective-permute-start | bytes 1958408 | tf_op jit(solution)/shard_map/ppermute | solution.py:36
  405.8 35.6 %collective-permute-start.23 = (bf16[912,200]{1,0:T(8,128)(2,1)S(1)}, bf16[912,200]{1,0:T(8,128)(2,1)S(1)}, u32[]{:S(2)}, u32[]{:S(2)}) collective-permute-start(bf16[912,200]{1,0:T(8,128)(2,1)S(1)} %get-tuple-element.87), channel_id=1, source_target_pairs={{0,2},{1,3},{2,0},{3,1},{4,6},{5,7},{6,4},{7,5},{8,10},{9,11},{10,... | collective-permute-start | bytes 1094408 | tf_op jit(solution)/shard_map/ppermute | solution.py:25
  409.9 31.6 %collective-permute-start.24 = (bf16[912,200]{1,0:T(8,128)(2,1)S(1)}, bf16[912,200]{1,0:T(8,128)(2,1)S(1)}, u32[]{:S(2)}, u32[]{:S(2)}) collective-permute-start(bf16[912,200]{1,0:T(8,128)(2,1)S(1)} %get-tuple-element.88), channel_id=1, source_target_pairs={{0,3},{1,2},{2,1},{3,0},{4,7},{5,6},{6,5},{7,4},{8,11},{9,10},{10,... | collective-permute-start | bytes 1094408 | tf_op jit(solution)/shard_map/ppermute | solution.py:25
  409.9 32.0 %collective-permute-start.47 = (bf16[208,800]{1,0:T(8,128)(2,1)}, bf16[208,800]{1,0:T(8,128)(2,1)}, u32[]{:S(2)}, u32[]{:S(2)}) collective-permute-start(bf16[208,800]{1,0:T(8,128)(2,1)} %slice_select_fusion.refs_0_), channel_id=1, source_target_pairs={{0,16},{1,17},{2,18},{3,19},{4,12},{5,13},{6,14},{7,15},{8,24},{9,... | collective-permute-start | bytes 998408 | tf_op jit(solution)/shard_map/ppermute | solution.py:36
  411.1 30.9 %collective-permute-start.48 = (bf16[208,800]{1,0:T(8,128)(2,1)}, bf16[208,800]{1,0:T(8,128)(2,1)}, u32[]{:S(2)}, u32[]{:S(2)}) collective-permute-start(bf16[208,800]{1,0:T(8,128)(2,1)} %collective-permute-done.46.refs_1_), channel_id=1, source_target_pairs={{0,16},{1,17},{2,18},{3,19},{4,12},{5,13},{6,14},{7,15},{8,24},{9,... | collective-permute-start | bytes 998408 | tf_op jit(solution)/shard_map/ppermute | solution.py:36
  (67 other events, 1034.6 us)
